TPU v7x, 512 devices: a whole 4x4x16 slice. The times are simulated.
512 devices in a mesh: space: 128 (over z, y, core), tm: 4 (over x).
Axes of the slice: x: 4, y: 4, z: 16, core: 2. Of those that a mesh axis runs over, the one named last changes fastest.
Arguments:
- snapshots: bfloat16 [262144, 2048], P('space', 'tm'), as said below
- sketch: bfloat16 [2048, 256], P('tm'), may hold values from -0.125 to 0.125
- rotation: float32 [256, 256], replicated, may hold values from -0.375 to 0.375
Outputs:
- basis: float32 [262144, 256], P(('space', 'tm'))
- triangle: float32 [256, 256], replicated
Inputs may be any that keep to these rules, and one draw needn't show every extreme that they name: `snapshots`: the sketch has full column rank.
All inputs are finite; a program needn't handle non-finite values.
Results may differ from a plain program's by a relative error of at most 0.0003.
Values sent between devices are 32-bit elements; how exact they have to be, the bound alone decides.
A program may use at most 64 MiB of HBM per device.

v0:
```python
import jax
import jax.numpy as jnp
from jax import lax
from jax.sharding import PartitionSpec as P


def shards(snapshots, sketch, rotation):
    sketched = lax.psum_scatter(
        jnp.dot(snapshots, sketch, preferred_element_type=jnp.float32),
        "tm",
        scatter_dimension=0,
        tiled=True,
    )
    gram = lax.dot_general(
        sketched,
        sketched,
        (((0,), (0,)), ((), ())),
        precision=lax.Precision.HIGHEST,
        preferred_element_type=jnp.float32,
    )
    gram = lax.psum(gram, ("space", "tm"))
    lower = jnp.linalg.cholesky(gram)
    orthonormal = lax.linalg.triangular_solve(
        lower, sketched, left_side=False, lower=True, transpose_a=True
    )
    cell_count = sketched.shape[0] * lax.axis_size("space") * lax.axis_size("tm")
    scale = jnp.sqrt(jnp.float32(cell_count))
    basis = scale * jnp.dot(
        orthonormal, rotation, precision=lax.Precision.HIGHEST, preferred_element_type=jnp.float32
    )
    triangle = lower.T / scale
    return (basis, triangle)


def solution(mesh):
    in_specs = (P("space", "tm"), P("tm", None), P())
    out_specs = (P(("space", "tm"), None), P())
    return jax.shard_map(shards, mesh=mesh, in_specs=in_specs, out_specs=out_specs, check_vma=False)
```

profile of v0, /device:TPU:1, one launch (start us, length us, event | category | flops | bytes accessed | tf_op | source)
XLA Modules:
  0.0 592.0 jit_solution(8189028408867632442)
XLA Ops:
  7.2 0.0 copy-start
  7.2 0.0 reduce-scatter.2.cloned.1.call-start
  7.2 1.5 copy-done
  8.8 3.0 fusion.14
  11.8 0.0 reduce-scatter.2.cloned.1.call-update
  11.8 0.0 all-reduce.3.cloned.1.call-start
  11.8 42.8 %reduce-scatter.2.cloned.1.call-done = f32[512,256]{1,0:T(8,128)} async-done(((f32[2048,256]{1,0:T(8,128)}), f32[512,256]{1,0:T(8,128)}) %reduce-scatter.2.cloned.1.call-update) | async-done | bytes 524304 | tf_op jit(solution)/shard_map/reduce_scatter | solution.py:8
  54.6 2.9 fusion.15
  57.5 0.0 all-reduce.3.cloned.1.call-update
  57.6 0.0 copy-start.1
  57.6 459.1 %all-reduce.3.cloned.1.call-done = f32[256,256]{0,1:T(8,128)} async-done(((f32[256,256]{0,1:T(8,128)}), f32[256,256]{0,1:T(8,128)}) %all-reduce.3.cloned.1.call-update) | async-done | bytes 262160 | tf_op jit(solution)/shard_map/psum | solution.py:21
  516.6 1.1 copy.6
  517.7 1.0 fusion.5
  518.7 11.7 %cholesky.50 = f32[128,128]{1,0:T(8,128)S(1)} custom-call(f32[128,128]{1,0:T(8,128)S(1)} %cholesky.118), custom_call_target="Cholesky" | custom-call | tf_op jit(solution)/shard_map/jit(cholesky)/cholesky | solution.py:22
  530.5 9.8 %custom-call.14 = f32[1,128,128]{1,2,0:T(8,128)S(1)} custom-call(f32[1,128,128]{2,1,0:T(8,128)S(1)} %get-tuple-element.27), custom_call_target="InvertDiagBlocksLowerTriangular" | custom-call | tf_op jit(solution)/shard_map/jit(cholesky)/cholesky | solution.py:22
  540.3 0.2 constant_dynamic-update-slice_fusion.1
  540.5 0.3 convolution_subtract_fusion.1
  540.8 11.7 %cholesky.105 = f32[128,128]{1,0:T(8,128)S(1)} custom-call(f32[128,128]{1,0:T(8,128)S(1)} %convolution_subtract_fusion.1), custom_call_target="Cholesky" | custom-call | tf_op jit(solution)/shard_map/jit(cholesky)/cholesky | solution.py:22
  552.5 0.7 compare_reduce_fusion
  554.7 0.1 triangular_solve.58
  554.7 4.2 while.1
  554.9 0.6 fusion.26
  555.5 1.4 bitcast_dynamic-update-slice_fusion.2
  556.9 0.6 fusion.26
  557.5 1.4 bitcast_dynamic-update-slice_fusion.2
  559.0 0.0 copy-start.2
  559.0 0.6 copy-done.2
  559.6 20.5 %custom-call.15 = f32[2,128,128]{1,2,0:T(8,128)S(1)} custom-call(f32[2,128,128]{2,1,0:T(8,128)} %copy-done.2), custom_call_target="InvertDiagBlocksLowerTriangular" | custom-call | tf_op jit(solution)/shard_map/triangular_solve | solution.py:23
  580.1 0.0 copy-done.1
  580.1 0.4 fusion.3
  580.5 0.6 convolution_subtract_fusion
  581.1 0.4 fusion.7
  581.6 0.8 copy.7
  582.4 2.7 convolution_multiply_fusion
  (9 shorter events, 0.2 us)
Async XLA Ops:
  7.2 1.6 copy-start
  7.2 47.4 %reduce-scatter.2.cloned.1.call-start = ((), (), s32[]{:S(2)}) async-start(), calls=%async_computation.1 | async-start | bytes 2621440 | tf_op jit(solution)/shard_map/reduce_scatter | solution.py:8
  11.8 504.8 %all-reduce.3.cloned.1.call-start = ((), (), s32[]{:S(2)}) async-start(), calls=%async_computation.2 | async-start | bytes 524288 | tf_op jit(solution)/shard_map/psum | solution.py:21
  57.6 522.6 %copy-start.1 = (f32[512,256]{1,0:T(8,128)S(1)}, f32[512,256]{1,0:T(8,128)}, u32[]{:S(2)}) copy-start(f32[512,256]{1,0:T(8,128)} %reduce-scatter.2.cloned.1.call-done) | copy-start | bytes 1572868
  559.0 0.7 copy-start.2
Sparse Core Ops, SparseCore 0:
  11.9 42.6 reduce-scatter.1
  61.5 455.0 all-reduce.2
where the time goes:
time: 593 us; the launch traced here: 592 us
  waiting for transfers between devices  502 us (85%)
  other arithmetic  55.5 us (9%)
  between operations  15.5 us (3%)
  matrix products  10.5 us (2%)
  local copies, waits for them, and re-layouts  8.27 us (1%)
    psum x1, waiting for transfers between devices, shards(): gram = lax.psum(gram, ('space', 'tm'))  459 us
    reduce_scatter x1, waiting for transfers between devices, shards(): lax.psum_scatter(jnp.dot(snapshots, sketch, preferred_element_type=jnp.fl...  42.8 us
    another operation x6, other arithmetic, shards(): lower = jnp.linalg.cholesky(gram)  34 us
    another operation x2, other arithmetic, shards(): lax.linalg.triangular_solve(lower, sketched, left_side=False, lower=True,...  20.5 us
  transfers between devices with their start and end apart: 2, of which 2 were waited for; matrix products, arithmetic and copies ran while one was open for 0% of the time, Pallas kernels for 0%

commit v1 on v0

v1 whole, which is shorter than its diff:
```python
import functools

import jax
import jax.numpy as jnp
from jax import lax
from jax.experimental import pallas as pl
from jax.experimental.pallas import tpu as pltpu
from jax.sharding import Mesh, PartitionSpec as P

MESH = pl.DeviceIdType.MESH
AXES = ("z", "y", "c", "x")
SPACE = ("z", "y", "c")
TILES = 64


def sum_kernel(sizes, a_ref, o_ref, zbuf, zsum, ybuf, ysum, xbuf, xsum, cbuf, full,
               zr, zs, yr, ys, xr, xs, cr, cs, ygr, ygs, zgr, zgs):
    nz, ny, nc, nx = sizes
    zi, yi, ci, xi = (lax.axis_index(a) for a in AXES)
    cz = TILES // nz
    cy = cz // ny

    def peers(n, me):
        return [lax.rem(me + d, n) for d in range(1, n)]

    barrier = pltpu.get_barrier_semaphore()
    count = 0
    for n, me, make in (
        (nz, zi, lambda j: (j, yi, ci, xi)),
        (ny, yi, lambda j: (zi, j, ci, xi)),
        (nc, ci, lambda j: (zi, yi, j, xi)),
        (nx, xi, lambda j: (zi, yi, ci, j)),
    ):
        for j in peers(n, me):
            pl.semaphore_signal(barrier, inc=1, device_id=make(j), device_id_type=MESH)
            count += 1
    pl.semaphore_wait(barrier, count)

    def exchange(n, me, make, src_of, dst_of, rsem, ssem):
        copies = []
        for j in peers(n, me):
            cp = pltpu.make_async_remote_copy(
                src_ref=src_of(j), dst_ref=dst_of(me), send_sem=ssem.at[j],
                recv_sem=rsem.at[me], device_id=make(j), device_id_type=MESH)
            cp.start()
            copies.append(cp)
        for j in peers(n, me):
            pltpu.make_async_remote_copy(
                src_ref=src_of(j), dst_ref=dst_of(j), send_sem=ssem.at[j],
                recv_sem=rsem.at[j], device_id=make(j), device_id_type=MESH).wait_recv()
        for cp in copies:
            cp.wait_send()

    def ordered_sum(buf, n):
        acc = buf[0]
        for j in range(1, n):
            acc = acc + buf[j]
        return acc

    zbuf[zi] = a_ref[pl.ds(zi * cz, cz)]
    exchange(nz, zi, lambda j: (j, yi, ci, xi),
             lambda j: a_ref.at[pl.ds(j * cz, cz)], lambda j: zbuf.at[j], zr, zs)
    zsum[...] = ordered_sum(zbuf, nz)

    ybuf[yi] = zsum[pl.ds(yi * cy, cy)]
    exchange(ny, yi, lambda j: (zi, j, ci, xi),
             lambda j: zsum.at[pl.ds(j * cy, cy)], lambda j: ybuf.at[j], yr, ys)
    ysum[...] = ordered_sum(ybuf, ny)

    xbuf[xi] = ysum[...]
    exchange(nx, xi, lambda j: (zi, yi, ci, j), lambda j: ysum, lambda j: xbuf.at[j], xr, xs)
    xsum[...] = ordered_sum(xbuf, nx)

    cbuf[ci] = xsum[...]
    exchange(nc, ci, lambda j: (zi, yi, j, xi), lambda j: xsum, lambda j: cbuf.at[j], cr, cs)
    own = zi * cz + yi * cy
    full[pl.ds(own, cy)] = ordered_sum(cbuf, nc)

    exchange(ny, yi, lambda j: (zi, j, ci, xi),
             lambda j: full.at[pl.ds(own, cy)],
             lambda j: full.at[pl.ds(zi * cz + j * cy, cy)], ygr, ygs)
    exchange(nz, zi, lambda j: (j, yi, ci, xi),
             lambda j: full.at[pl.ds(zi * cz, cz)],
             lambda j: full.at[pl.ds(j * cz, cz)], zgr, zgs)
    o_ref[...] = full[...]


def all_sum(gram, sizes):
    nz, ny, nc, nx = sizes
    cz = TILES // nz
    cy = cz // ny
    rows, cols = gram.shape
    tiles = gram.reshape(TILES, (rows * cols) // (TILES * 128), 128)
    t = tiles.shape[1:]
    dma = pltpu.SemaphoreType.DMA
    out = pl.pallas_call(
        functools.partial(sum_kernel, sizes),
        out_shape=jax.ShapeDtypeStruct(tiles.shape, jnp.float32),
        in_specs=[pl.BlockSpec(memory_space=pltpu.VMEM)],
        out_specs=pl.BlockSpec(memory_space=pltpu.VMEM),
        scratch_shapes=[
            pltpu.VMEM((nz, cz) + t, jnp.float32),
            pltpu.VMEM((cz,) + t, jnp.float32),
            pltpu.VMEM((ny, cy) + t, jnp.float32),
            pltpu.VMEM((cy,) + t, jnp.float32),
            pltpu.VMEM((nx, cy) + t, jnp.float32),
            pltpu.VMEM((cy,) + t, jnp.float32),
            pltpu.VMEM((nc, cy) + t, jnp.float32),
            pltpu.VMEM(tiles.shape, jnp.float32),
            dma((nz,)), dma((nz,)), dma((ny,)), dma((ny,)),
            dma((nx,)), dma((nx,)), dma((nc,)), dma((nc,)),
            dma((ny,)), dma((ny,)), dma((nz,)), dma((nz,)),
        ],
        compiler_params=pltpu.CompilerParams(collective_id=0, has_side_effects=True),
    )(tiles)
    return out.reshape(rows, cols)


def shards(sizes, snapshots, sketch, rotation):
    sketched = lax.psum_scatter(
        jnp.dot(snapshots, sketch, preferred_element_type=jnp.float32),
        "x",
        scatter_dimension=0,
        tiled=True,
    )
    gram = lax.dot_general(
        sketched,
        sketched,
        (((0,), (0,)), ((), ())),
        precision=lax.Precision.HIGHEST,
        preferred_element_type=jnp.float32,
    )
    gram = all_sum(gram, sizes)
    lower = jnp.linalg.cholesky(gram)
    orthonormal = lax.linalg.triangular_solve(
        lower, sketched, left_side=False, lower=True, transpose_a=True
    )
    cell_count = sketched.shape[0] * sizes[0] * sizes[1] * sizes[2] * sizes[3]
    scale = jnp.sqrt(jnp.float32(cell_count))
    basis = scale * jnp.dot(
        orthonormal, rotation, precision=lax.Precision.HIGHEST, preferred_element_type=jnp.float32
    )
    triangle = lower.T / scale
    return (basis, triangle)


def physical_mesh(mesh):
    space, tm = mesh.devices.shape
    nc = 2
    ny = 4 if space % 8 == 0 else 1
    nz = space // (ny * nc)
    devs = mesh.devices.reshape(nz, ny, nc, tm)
    return Mesh(devs, AXES), (nz, ny, nc, tm)


def solution(mesh):
    m4, sizes = physical_mesh(mesh)
    in_specs = (P(SPACE, "x"), P("x", None), P())
    out_specs = (P(AXES, None), P())
    return jax.shard_map(functools.partial(shards, sizes), mesh=m4, in_specs=in_specs,
                         out_specs=out_specs, check_vma=False)
```

time: 593 us -> 186 us (0.31)
  waiting for transfers between devices: 502 us -> 42.8 us
  Pallas kernels: 0 us -> 53.8 us
    psum x1 -> x0, waiting for transfers between devices: 459 us -> none  [shards(): gram = lax.psum(gram, ('space', 'tm'))]
    pallas_call x0 -> x1, Pallas kernels: none -> 53.8 us  [all_sum(): pl.pallas_call(functools.partial(sum_kernel, sizes), out_shape=jax.ShapeD...]
  transfers between devices with their start and end apart: 2 -> 1, of which waited for: 2 -> 1; matrix products, arithmetic and copies ran while one was open for 0% -> 0% of each run, Pallas kernels for 0% -> 0%
where the time goes in v1:
time: 186 us
  other arithmetic  54.7 us (29%)
  Pallas kernels  53.8 us (29%)
  waiting for transfers between devices  42.8 us (23%)
  between operations  15.5 us (8%)
  matrix products  9.83 us (5%)
  local copies, waits for them, and re-layouts  9.07 us (5%)
    pallas_call x1, Pallas kernels, all_sum(): pl.pallas_call(functools.partial(sum_kernel, sizes), out_shape=jax.ShapeD...  53.8 us
    reduce_scatter x1, waiting for transfers between devices, shards(): lax.psum_scatter(jnp.dot(snapshots, sketch, preferred_element_type=jnp.fl...  42.8 us
    another operation x6, other arithmetic, shards(): lower = jnp.linalg.cholesky(gram)  34.2 us
    another operation x2, other arithmetic, shards(): lax.linalg.triangular_solve(lower, sketched, left_side=False, lower=True,...  20.5 us
    another operation x6, local copies, waits for them, and re-layouts  4.06 us
  transfers between devices with their start and end apart: 1, of which 1 were waited for; matrix products, arithmetic and copies ran while one was open for 0% of the time, Pallas kernels for 0%

profile of v1, /device:TPU:1, one launch (start us, length us, event | category | flops | bytes accessed | tf_op | source)
XLA Modules:
  0.0 185.9 jit_solution(12013062660035596368)
XLA Ops:
  7.2 0.0 copy-start
  7.2 0.0 reduce-scatter.2.cloned.1.call-start
  7.2 1.5 copy-done
  8.8 3.0 %fusion.14 = f32[2048,256]{1,0:T(8,128)} fusion(bf16[2048,512]{1,0:T(8,128)(2,1)S(1)} %copy-done, bf16[512,256]{1,0:T(8,128)(2,1)} %param.4), kind=kOutput, calls=%fused_computation.35 | convolution fusion | flops 536870912 | bytes 4456448 | tf_op jit(solution)/shard_map/dot_general | solution.py:121
  11.8 0.0 reduce-scatter.2.cloned.1.call-update
  11.8 42.8 %reduce-scatter.2.cloned.1.call-done = f32[512,256]{1,0:T(8,128)} async-done(((f32[2048,256]{1,0:T(8,128)}), f32[512,256]{1,0:T(8,128)}) %reduce-scatter.2.cloned.1.call-update) | async-done | bytes 524304 | tf_op jit(solution)/shard_map/reduce_scatter | solution.py:120
  54.6 2.2 %fusion.15 = f32[256,256]{1,0:T(8,128)S(1)} fusion(f32[512,256]{1,0:T(8,128)} %reduce-scatter.2.cloned.1.call-done), kind=kOutput, calls=%fused_computation.36 | convolution fusion | flops 402653184 | bytes 786432 | tf_op jit(solution)/shard_map/dot_general | solution.py:126
  56.8 0.7 reshape.27.a_ref
  57.6 53.8 %shard_map.50 = f32[64,8,128]{2,1,0:T(8,128)} custom-call(f32[64,8,128]{2,1,0:T(8,128)} %reshape.27.a_ref), custom_call_target="tpu_custom_call" | custom-call | tf_op jit(solution)/shard_map/pallas_call | solution.py:96
  111.4 1.0 reshape.28
  112.4 0.0 copy-start.1
  112.4 0.1 copy.7
  112.6 11.7 %cholesky.50 = f32[128,128]{1,0:T(8,128)S(1)} custom-call(f32[128,128]{1,0:T(8,128)S(1)} %cholesky.118), custom_call_target="Cholesky" | custom-call | tf_op jit(solution)/shard_map/jit(cholesky)/cholesky | solution.py:134
  124.3 9.8 %custom-call.14 = f32[1,128,128]{1,2,0:T(8,128)S(1)} custom-call(f32[1,128,128]{2,1,0:T(8,128)S(1)} %get-tuple-element.29), custom_call_target="InvertDiagBlocksLowerTriangular" | custom-call | tf_op jit(solution)/shard_map/jit(cholesky)/cholesky | solution.py:134
  134.2 0.2 constant_dynamic-update-slice_fusion.1
  134.4 0.3 convolution_subtract_fusion.1
  134.7 11.8 %cholesky.105 = f32[128,128]{1,0:T(8,128)S(1)} custom-call(f32[128,128]{1,0:T(8,128)S(1)} %convolution_subtract_fusion.1), custom_call_target="Cholesky" | custom-call | tf_op jit(solution)/shard_map/jit(cholesky)/cholesky | solution.py:134
  146.6 0.7 compare_reduce_fusion
  148.7 0.1 triangular_solve.58
  148.7 4.1 %while.1 = (s32[]{:T(128)}, f32[256,256]{1,0:T(8,128)S(1)}, s32[2,2]{1,0:T(2,128)S(1)}, f32[2,128,128]{2,1,0:T(8,128)S(1)}, s32[]{:T(128)}) while((s32[]{:T(128)}, f32[256,256]{1,0:T(8,128)S(1)}, s32[2,2]{1,0:T(2,128)S(1)}, f32[2,128,128]{2,1,0:T(8,128)S(1)}, s32[]{:T(128)}) %tuple.30), condition=%wide.while_cond, body=%wide.while_body.sunk | while | flops 2 | bytes 131181 | solution.py:135
  148.7 0.6 fusion.26
  149.3 1.4 bitcast_dynamic-update-slice_fusion.2
  150.8 0.6 fusion.26
  151.4 1.4 bitcast_dynamic-update-slice_fusion.2
  152.8 0.0 copy-start.2
  152.9 0.6 copy-done.2
  153.5 20.5 %custom-call.15 = f32[2,128,128]{1,2,0:T(8,128)S(1)} custom-call(f32[2,128,128]{2,1,0:T(8,128)} %copy-done.2), custom_call_target="InvertDiagBlocksLowerTriangular" | custom-call | tf_op jit(solution)/shard_map/triangular_solve | solution.py:135
  174.0 0.0 copy-done.1
  174.0 0.4 fusion.3
  174.4 0.6 convolution_subtract_fusion
  175.0 0.4 fusion.7
  175.4 0.8 copy.8
  176.3 2.7 %convolution_multiply_fusion = f32[512,256]{1,0:T(8,128)} fusion(f32[256,256]{1,0:T(8,128)} %param.5, f32[512,128]{0,1:T(8,128)S(1)} %fusion.7, f32[512,128]{0,1:T(8,128)S(1)} %fusion.3), kind=kOutput, calls=%fused_computation.2 | convolution fusion | flops 402915328 | bytes 1310720 | tf_op jit(solution)/shard_map/dot_general | solution.py:140
  (10 shorter events, 0.2 us)
Async XLA Ops:
  7.2 1.6 copy-start
  7.2 47.4 %reduce-scatter.2.cloned.1.call-start = ((), (), s32[]{:S(2)}) async-start(), calls=%async_computation.1 | async-start | bytes 2621440 | tf_op jit(solution)/shard_map/reduce_scatter | solution.py:120
  112.4 61.6 %copy-start.1 = (f32[512,256]{1,0:T(8,128)S(1)}, f32[512,256]{1,0:T(8,128)}, u32[]{:S(2)}) copy-start(f32[512,256]{1,0:T(8,128)} %reduce-scatter.2.cloned.1.call-done) | copy-start | bytes 1572868
  152.8 0.7 copy-start.2
Sparse Core Ops, SparseCore 0:
  11.9 42.6 reduce-scatter.1

commit v2 on v1

--- a/solution.py
+++ b/solution.py
@@ -116,13 +116,63 @@
     return out.reshape(rows, cols)
 
 
+def scatter_kernel(nx, s_ref, k_ref, o_ref, part, rbuf, rs, ss):
+    xi = lax.axis_index("x")
+    rows = o_ref.shape[0]
+
+    barrier = pltpu.get_barrier_semaphore()
+    for d in range(1, nx):
+        pl.semaphore_signal(barrier, inc=1, device_id={"x": lax.rem(xi + d, nx)},
+                            device_id_type=MESH)
+    pl.semaphore_wait(barrier, nx - 1)
+
+    copies = []
+    for d in range(1, nx):
+        j = lax.rem(xi + d, nx)
+        block = s_ref[pl.ds(pl.multiple_of(j * rows, rows), rows), :]
+        part[j] = jnp.dot(block, k_ref[...], preferred_element_type=jnp.float32)
+        cp = pltpu.make_async_remote_copy(
+            src_ref=part.at[j], dst_ref=rbuf.at[xi], send_sem=ss.at[j],
+            recv_sem=rs.at[xi], device_id={"x": j}, device_id_type=MESH)
+        cp.start()
+        copies.append(cp)
+    block = s_ref[pl.ds(pl.multiple_of(xi * rows, rows), rows), :]
+    rbuf[xi] = jnp.dot(block, k_ref[...], preferred_element_type=jnp.float32)
+    for d in range(1, nx):
+        j = lax.rem(xi + d, nx)
+        pltpu.make_async_remote_copy(
+            src_ref=part.at[j], dst_ref=rbuf.at[j], send_sem=ss.at[j],
+            recv_sem=rs.at[j], device_id={"x": j}, device_id_type=MESH).wait_recv()
+    acc = rbuf[0]
+    for j in range(1, nx):
+        acc = acc + rbuf[j]
+    o_ref[...] = acc
+    for cp in copies:
+        cp.wait_send()
+
+
+def sketch_scatter(snapshots, sketch, nx):
+    cells = snapshots.shape[0]
+    rows = cells // nx
+    cols = sketch.shape[1]
+    dma = pltpu.SemaphoreType.DMA
+    return pl.pallas_call(
+        functools.partial(scatter_kernel, nx),
+        out_shape=jax.ShapeDtypeStruct((rows, cols), jnp.float32),
+        in_specs=[pl.BlockSpec(memory_space=pltpu.VMEM)] * 2,
+        out_specs=pl.BlockSpec(memory_space=pltpu.VMEM),
+        scratch_shapes=[
+            pltpu.VMEM((nx, rows, cols), jnp.float32),
+            pltpu.VMEM((nx, rows, cols), jnp.float32),
+            dma((nx,)), dma((nx,)),
+        ],
+        compiler_params=pltpu.CompilerParams(collective_id=1, has_side_effects=True,
+                                             vmem_limit_bytes=48 * 1024 * 1024),
+    )(snapshots, sketch)
+
+
 def shards(sizes, snapshots, sketch, rotation):
-    sketched = lax.psum_scatter(
-        jnp.dot(snapshots, sketch, preferred_element_type=jnp.float32),
-        "x",
-        scatter_dimension=0,
-        tiled=True,
-    )
+    sketched = sketch_scatter(snapshots, sketch, sizes[3])
     gram = lax.dot_general(
         sketched,
         sketched,

time: 186 us -> 157 us (0.84)
  waiting for transfers between devices: 42.8 us -> 0 us
  Pallas kernels: 53.8 us -> 86.6 us
  between operations: 15.5 us -> 2.12 us
  matrix products: 9.83 us -> 4.71 us
    reduce_scatter x1 -> x0, waiting for transfers between devices: 42.8 us -> none  [shards(): lax.psum_scatter(jnp.dot(snapshots, sketch, preferred_element_type=jnp.fl...]
    pallas_call x0 -> x1, Pallas kernels: none -> 28.1 us  [sketch_scatter(): pl.pallas_call(functools.partial(scatter_kernel, nx), out_shape=jax.Shape...]
    pallas_call x1, Pallas kernels: 53.8 us -> 58.5 us  [all_sum(): pl.pallas_call(functools.partial(sum_kernel, sizes), out_shape=jax.ShapeD...]
    dot_general x1 -> x0, matrix products: 3 us -> none  [shards(): jnp.dot(snapshots, sketch, preferred_element_type=jnp.float32)]
  transfers between devices with their start and end apart: 1 -> 0, of which waited for: 1 -> 0; matrix products, arithmetic and copies ran while one was open for 0% -> 0% of each run, Pallas kernels for 0% -> 0%
where the time goes in v2:
time: 157 us
  Pallas kernels  86.6 us (55%)
  other arithmetic  54 us (34%)
  local copies, waits for them, and re-layouts  9.38 us (6%)
  matrix products  4.71 us (3%)
  between operations  2.12 us (1%)
    pallas_call x1, Pallas kernels, all_sum(): pl.pallas_call(functools.partial(sum_kernel, sizes), out_shape=jax.ShapeD...  58.5 us
    another operation x6, other arithmetic, shards(): lower = jnp.linalg.cholesky(gram)  34.2 us
    pallas_call x1, Pallas kernels, sketch_scatter(): pl.pallas_call(functools.partial(scatter_kernel, nx), out_shape=jax.Shape...  28.1 us
    another operation x2, other arithmetic, shards(): lax.linalg.triangular_solve(lower, sketched, left_side=False, lower=True,...  19.7 us
    another operation x6, local copies, waits for them, and re-layouts  4.02 us
    unnamed x7, local copies, waits for them, and re-layouts  3.39 us

profile of v2, /device:TPU:1, one launch (start us, length us, event | category | flops | bytes accessed | tf_op | source)
XLA Modules:
  0.0 156.8 jit_solution(9503417383570209260)
XLA Ops:
  0.6 0.0 copy-start
  0.7 0.1 triangular_solve.58
  0.7 0.0 copy-start.1
  0.7 1.6 %copy-done.1 = bf16[2048,512]{1,0:T(8,128)(2,1)S(1)} copy-done((bf16[2048,512]{1,0:T(8,128)(2,1)S(1)}, bf16[2048,512]{1,0:T(8,128)(2,1)}, u32[]{:S(2)}) %copy-start.1) | copy-done | bytes 2097176
  2.3 0.0 copy-start.2
  2.3 0.9 copy-done.2
  3.3 28.1 %shard_map.50 = f32[512,256]{1,0:T(8,128)S(1)} custom-call(bf16[2048,512]{1,0:T(8,128)(2,1)S(1)} %copy-done.1, bf16[512,256]{1,0:T(8,128)(2,1)S(1)} %copy-done.2), custom_call_target="tpu_custom_call" | custom-call | tf_op jit(solution)/shard_map/pallas_call | solution.py:159
  31.4 1.0 fusion.14
  32.4 0.7 reshape.27.a_ref
  33.1 58.5 %shard_map.51 = f32[64,8,128]{2,1,0:T(8,128)} custom-call(f32[64,8,128]{2,1,0:T(8,128)} %reshape.27.a_ref), custom_call_target="tpu_custom_call" | custom-call | tf_op jit(solution)/shard_map/pallas_call | solution.py:96
  91.7 1.0 reshape.28
  92.7 0.1 copy.7
  92.9 11.7 %cholesky.50 = f32[128,128]{1,0:T(8,128)S(1)} custom-call(f32[128,128]{1,0:T(8,128)S(1)} %cholesky.118), custom_call_target="Cholesky" | custom-call | tf_op jit(solution)/shard_map/jit(cholesky)/cholesky | solution.py:184
  104.6 9.8 %custom-call.14 = f32[1,128,128]{1,2,0:T(8,128)S(1)} custom-call(f32[1,128,128]{2,1,0:T(8,128)S(1)} %get-tuple-element.29), custom_call_target="InvertDiagBlocksLowerTriangular" | custom-call | tf_op jit(solution)/shard_map/jit(cholesky)/cholesky | solution.py:184
  114.5 0.2 constant_dynamic-update-slice_fusion.1
  114.7 0.3 convolution_subtract_fusion.1
  115.0 11.9 %cholesky.105 = f32[128,128]{1,0:T(8,128)S(1)} custom-call(f32[128,128]{1,0:T(8,128)S(1)} %convolution_subtract_fusion.1), custom_call_target="Cholesky" | custom-call | tf_op jit(solution)/shard_map/jit(cholesky)/cholesky | solution.py:184
  126.9 0.7 compare_reduce_fusion
  129.0 0.8 copy.8
  129.8 4.1 %while.1 = (s32[]{:T(128)}, f32[256,256]{1,0:T(8,128)S(1)}, s32[2,2]{1,0:T(2,128)S(1)}, f32[2,128,128]{2,1,0:T(8,128)S(1)}, s32[]{:T(128)}) while((s32[]{:T(128)}, f32[256,256]{1,0:T(8,128)S(1)}, s32[2,2]{1,0:T(2,128)S(1)}, f32[2,128,128]{2,1,0:T(8,128)S(1)}, s32[]{:T(128)}) %tuple.30), condition=%wide.while_cond, body=%wide.while_body.sunk | while | flops 2 | bytes 131189 | solution.py:185
  129.8 0.7 fusion.23
  130.5 1.3 bitcast_dynamic-update-slice_fusion.2
  131.9 0.7 fusion.23
  132.5 1.3 bitcast_dynamic-update-slice_fusion.2
  133.9 19.7 %custom-call.15 = f32[2,128,128]{1,2,0:T(8,128)S(1)} custom-call(f32[2,128,128]{2,1,0:T(8,128)S(1)} %get-tuple-element.9), custom_call_target="InvertDiagBlocksLowerTriangular" | custom-call | tf_op jit(solution)/shard_map/triangular_solve | solution.py:185
  153.6 0.4 fusion.5
  154.0 0.6 convolution_subtract_fusion
  154.6 0.4 fusion.7
  155.0 0.0 copy-done
  155.0 1.8 %convolution_multiply_fusion = f32[512,256]{1,0:T(8,128)} fusion(f32[256,256]{1,0:T(8,128)S(1)} %copy-done, f32[512,128]{0,1:T(8,128)S(1)} %fusion.7, f32[512,128]{0,1:T(8,128)S(1)} %fusion.5), kind=kOutput, calls=%fused_computation.2 | convolution fusion | flops 402915328 | bytes 1310720 | tf_op jit(solution)/shard_map/dot_general | solution.py:190
  (10 shorter events, 0.2 us)
Async XLA Ops:
  0.6 154.4 %copy-start = (f32[256,256]{1,0:T(8,128)S(1)}, f32[256,256]{1,0:T(8,128)}, u32[]{:S(2)}) copy-start(f32[256,256]{1,0:T(8,128)} %param.5) | copy-start | bytes 786436
  0.7 1.6 %copy-start.1 = (bf16[2048,512]{1,0:T(8,128)(2,1)S(1)}, bf16[2048,512]{1,0:T(8,128)(2,1)}, u32[]{:S(2)}) copy-start(bf16[2048,512]{1,0:T(8,128)(2,1)} %s_ref.1) | copy-start | bytes 6291460
  2.3 0.9 copy-start.2

commit v3 on v2

--- a/solution.py
+++ b/solution.py
@@ -182,13 +182,13 @@
     )
     gram = all_sum(gram, sizes)
     lower = jnp.linalg.cholesky(gram)
-    orthonormal = lax.linalg.triangular_solve(
-        lower, sketched, left_side=False, lower=True, transpose_a=True
+    rotated = lax.linalg.triangular_solve(
+        lower, rotation, left_side=True, lower=True, transpose_a=True
     )
     cell_count = sketched.shape[0] * sizes[0] * sizes[1] * sizes[2] * sizes[3]
     scale = jnp.sqrt(jnp.float32(cell_count))
     basis = scale * jnp.dot(
-        orthonormal, rotation, precision=lax.Precision.HIGHEST, preferred_element_type=jnp.float32
+        sketched, rotated, precision=lax.Precision.HIGHEST, preferred_element_type=jnp.float32
     )
     triangle = lower.T / scale
     return (basis, triangle)

time: 157 us -> 156 us (level)
  no operation moved by 1% of the time
where the time goes in v3:
time: 156 us
  Pallas kernels  86.6 us (56%)
  other arithmetic  53.9 us (35%)
  local copies, waits for them, and re-layouts  9.41 us (6%)
  matrix products  3.69 us (2%)
  between operations  2.09 us (1%)
    pallas_call x1, Pallas kernels, all_sum(): pl.pallas_call(functools.partial(sum_kernel, sizes), out_shape=jax.ShapeD...  58.5 us
    another operation x6, other arithmetic, shards(): lower = jnp.linalg.cholesky(gram)  34.1 us
    pallas_call x1, Pallas kernels, sketch_scatter(): pl.pallas_call(functools.partial(scatter_kernel, nx), out_shape=jax.Shape...  28.1 us
    another operation x2, other arithmetic, shards(): lax.linalg.triangular_solve(lower, rotation, left_side=True, lower=True,...  19.7 us
    another operation x6, local copies, waits for them, and re-layouts  4.06 us
    unnamed x7, local copies, waits for them, and re-layouts  3.38 us

profile of v3, /device:TPU:1, one launch (start us, length us, event | category | flops | bytes accessed | tf_op | source)
XLA Modules:
  0.0 155.7 jit_solution(12647110896332395280)
XLA Ops:
  0.6 0.0 copy-start
  0.6 1.6 %copy-done = bf16[2048,512]{1,0:T(8,128)(2,1)S(1)} copy-done((bf16[2048,512]{1,0:T(8,128)(2,1)S(1)}, bf16[2048,512]{1,0:T(8,128)(2,1)}, u32[]{:S(2)}) %copy-start) | copy-done | bytes 2097176
  2.2 0.0 copy-start.1
  2.2 0.9 copy-done.1
  3.2 28.1 %shard_map.50 = f32[512,256]{1,0:T(8,128)S(1)} custom-call(bf16[2048,512]{1,0:T(8,128)(2,1)S(1)} %copy-done, bf16[512,256]{1,0:T(8,128)(2,1)S(1)} %copy-done.1), custom_call_target="tpu_custom_call" | custom-call | tf_op jit(solution)/shard_map/pallas_call | solution.py:159
  31.3 1.0 fusion.14
  32.3 0.7 reshape.27.a_ref
  33.0 58.5 %shard_map.51 = f32[64,8,128]{2,1,0:T(8,128)} custom-call(f32[64,8,128]{2,1,0:T(8,128)} %reshape.27.a_ref), custom_call_target="tpu_custom_call" | custom-call | tf_op jit(solution)/shard_map/pallas_call | solution.py:96
  91.6 1.0 reshape.28
  92.6 0.0 copy-start.2
  92.6 0.1 copy.7
  92.8 11.7 %cholesky.50 = f32[128,128]{1,0:T(8,128)S(1)} custom-call(f32[128,128]{1,0:T(8,128)S(1)} %cholesky.118), custom_call_target="Cholesky" | custom-call | tf_op jit(solution)/shard_map/jit(cholesky)/cholesky | solution.py:184
  104.5 9.8 %custom-call.14 = f32[1,128,128]{1,2,0:T(8,128)S(1)} custom-call(f32[1,128,128]{2,1,0:T(8,128)S(1)} %get-tuple-element.29), custom_call_target="InvertDiagBlocksLowerTriangular" | custom-call | tf_op jit(solution)/shard_map/jit(cholesky)/cholesky | solution.py:184
  114.4 0.2 constant_dynamic-update-slice_fusion.1
  114.6 0.3 convolution_subtract_fusion.1
  114.9 11.9 %cholesky.105 = f32[128,128]{1,0:T(8,128)S(1)} custom-call(f32[128,128]{1,0:T(8,128)S(1)} %convolution_subtract_fusion.1), custom_call_target="Cholesky" | custom-call | tf_op jit(solution)/shard_map/jit(cholesky)/cholesky | solution.py:184
  126.8 0.6 compare_reduce_fusion
  128.8 0.1 triangular_solve.57
  128.9 4.1 %while.1 = (s32[]{:T(128)}, f32[256,256]{1,0:T(8,128)S(1)}, s32[2,2]{1,0:T(2,128)S(1)}, f32[2,128,128]{2,1,0:T(8,128)S(1)}, s32[]{:T(128)}) while((s32[]{:T(128)}, f32[256,256]{1,0:T(8,128)S(1)}, s32[2,2]{1,0:T(2,128)S(1)}, f32[2,128,128]{2,1,0:T(8,128)S(1)}, s32[]{:T(128)}) %tuple.30), condition=%wide.while_cond, body=%wide.while_body.sunk | while | flops 2 | bytes 131181 | solution.py:185
  128.9 0.6 fusion.23
  129.5 1.4 bitcast_dynamic-update-slice_fusion.2
  130.9 0.6 fusion.23
  131.5 1.4 bitcast_dynamic-update-slice_fusion.2
  133.0 19.7 %custom-call.15 = f32[2,128,128]{1,2,0:T(8,128)S(1)} custom-call(f32[2,128,128]{2,1,0:T(8,128)S(1)} %get-tuple-element.9), custom_call_target="InvertDiagBlocksLowerTriangular" | custom-call | tf_op jit(solution)/shard_map/triangular_solve | solution.py:185
  152.7 0.0 copy-done.2
  152.7 0.3 fusion.5
  152.9 0.3 convolution_subtract_fusion
  153.2 0.3 fusion.8
  153.5 1.4 convolution_multiply_fusion
  154.9 0.8 copy.8
  (10 shorter events, 0.2 us)
Async XLA Ops:
  0.6 1.6 %copy-start = (bf16[2048,512]{1,0:T(8,128)(2,1)S(1)}, bf16[2048,512]{1,0:T(8,128)(2,1)}, u32[]{:S(2)}) copy-start(bf16[2048,512]{1,0:T(8,128)(2,1)} %s_ref.1) | copy-start | bytes 6291460
  2.2 0.9 copy-start.1
  92.6 60.1 %copy-start.2 = (f32[256,256]{1,0:T(8,128)S(1)}, f32[256,256]{1,0:T(8,128)}, u32[]{:S(2)}) copy-start(f32[256,256]{1,0:T(8,128)} %param.5) | copy-start | bytes 786436

commit v4 on v3

--- a/solution.py
+++ b/solution.py
@@ -13,12 +13,10 @@
 TILES = 64
 
 
-def sum_kernel(sizes, a_ref, o_ref, zbuf, zsum, ybuf, ysum, xbuf, xsum, cbuf, full,
-               zr, zs, yr, ys, xr, xs, cr, cs, ygr, ygs, zgr, zgs):
+def sum_kernel(sizes, a_ref, o_ref, cbuf, csum, xbuf, xsum, ybuf, ysum, zbuf, full,
+               cr, cs, xr, xs, yr, ys, zr, zs, ygr, ygs, xgr, xgs, cgr, cgs):
     nz, ny, nc, nx = sizes
     zi, yi, ci, xi = (lax.axis_index(a) for a in AXES)
-    cz = TILES // nz
-    cy = cz // ny
 
     def peers(n, me):
         return [lax.rem(me + d, n) for d in range(1, n)]
@@ -57,38 +55,45 @@
             acc = acc + buf[j]
         return acc
 
-    zbuf[zi] = a_ref[pl.ds(zi * cz, cz)]
-    exchange(nz, zi, lambda j: (j, yi, ci, xi),
-             lambda j: a_ref.at[pl.ds(j * cz, cz)], lambda j: zbuf.at[j], zr, zs)
-    zsum[...] = ordered_sum(zbuf, nz)
-
-    ybuf[yi] = zsum[pl.ds(yi * cy, cy)]
-    exchange(ny, yi, lambda j: (zi, j, ci, xi),
-             lambda j: zsum.at[pl.ds(j * cy, cy)], lambda j: ybuf.at[j], yr, ys)
+    c1 = TILES // nc
+    c2 = c1 // nx
+    c3 = c2 // ny
+    zdev = lambda j: (j, yi, ci, xi)
+    ydev = lambda j: (zi, j, ci, xi)
+    cdev = lambda j: (zi, yi, j, xi)
+    xdev = lambda j: (zi, yi, ci, j)
+
+    cbuf[ci] = a_ref[pl.ds(ci * c1, c1)]
+    exchange(nc, ci, cdev, lambda j: a_ref.at[pl.ds(j * c1, c1)], lambda j: cbuf.at[j], cr, cs)
+    csum[...] = ordered_sum(cbuf, nc)
+
+    xbuf[xi] = csum[pl.ds(xi * c2, c2)]
+    exchange(nx, xi, xdev, lambda j: csum.at[pl.ds(j * c2, c2)], lambda j: xbuf.at[j], xr, xs)
+    xsum[...] = ordered_sum(xbuf, nx)
+
+    ybuf[yi] = xsum[pl.ds(yi * c3, c3)]
+    exchange(ny, yi, ydev, lambda j: xsum.at[pl.ds(j * c3, c3)], lambda j: ybuf.at[j], yr, ys)
     ysum[...] = ordered_sum(ybuf, ny)
 
-    xbuf[xi] = ysum[...]
-    exchange(nx, xi, lambda j: (zi, yi, ci, j), lambda j: ysum, lambda j: xbuf.at[j], xr, xs)
-    xsum[...] = ordered_sum(xbuf, nx)
-
-    cbuf[ci] = xsum[...]
-    exchange(nc, ci, lambda j: (zi, yi, j, xi), lambda j: xsum, lambda j: cbuf.at[j], cr, cs)
-    own = zi * cz + yi * cy
-    full[pl.ds(own, cy)] = ordered_sum(cbuf, nc)
-
-    exchange(ny, yi, lambda j: (zi, j, ci, xi),
-             lambda j: full.at[pl.ds(own, cy)],
-             lambda j: full.at[pl.ds(zi * cz + j * cy, cy)], ygr, ygs)
-    exchange(nz, zi, lambda j: (j, yi, ci, xi),
-             lambda j: full.at[pl.ds(zi * cz, cz)],
-             lambda j: full.at[pl.ds(j * cz, cz)], zgr, zgs)
+    zbuf[zi] = ysum[...]
+    exchange(nz, zi, zdev, lambda j: ysum, lambda j: zbuf.at[j], zr, zs)
+    own = ci * c1 + xi * c2 + yi * c3
+    full[pl.ds(own, c3)] = ordered_sum(zbuf, nz)
+
+    exchange(ny, yi, ydev, lambda j: full.at[pl.ds(own, c3)],
+             lambda j: full.at[pl.ds(ci * c1 + xi * c2 + j * c3, c3)], ygr, ygs)
+    exchange(nx, xi, xdev, lambda j: full.at[pl.ds(ci * c1 + xi * c2, c2)],
+             lambda j: full.at[pl.ds(ci * c1 + j * c2, c2)], xgr, xgs)
+    exchange(nc, ci, cdev, lambda j: full.at[pl.ds(ci * c1, c1)],
+             lambda j: full.at[pl.ds(j * c1, c1)], cgr, cgs)
     o_ref[...] = full[...]
 
 
 def all_sum(gram, sizes):
     nz, ny, nc, nx = sizes
-    cz = TILES // nz
-    cy = cz // ny
+    c1 = TILES // nc
+    c2 = c1 // nx
+    c3 = c2 // ny
     rows, cols = gram.shape
     tiles = gram.reshape(TILES, (rows * cols) // (TILES * 128), 128)
     t = tiles.shape[1:]
@@ -99,17 +104,18 @@
         in_specs=[pl.BlockSpec(memory_space=pltpu.VMEM)],
         out_specs=pl.BlockSpec(memory_space=pltpu.VMEM),
         scratch_shapes=[
-            pltpu.VMEM((nz, cz) + t, jnp.float32),
-            pltpu.VMEM((cz,) + t, jnp.float32),
-            pltpu.VMEM((ny, cy) + t, jnp.float32),
-            pltpu.VMEM((cy,) + t, jnp.float32),
-            pltpu.VMEM((nx, cy) + t, jnp.float32),
-            pltpu.VMEM((cy,) + t, jnp.float32),
-            pltpu.VMEM((nc, cy) + t, jnp.float32),
+            pltpu.VMEM((nc, c1) + t, jnp.float32),
+            pltpu.VMEM((c1,) + t, jnp.float32),
+            pltpu.VMEM((nx, c2) + t, jnp.float32),
+            pltpu.VMEM((c2,) + t, jnp.float32),
+            pltpu.VMEM((ny, c3) + t, jnp.float32),
+            pltpu.VMEM((c3,) + t, jnp.float32),
+            pltpu.VMEM((nz, c3) + t, jnp.float32),
             pltpu.VMEM(tiles.shape, jnp.float32),
-            dma((nz,)), dma((nz,)), dma((ny,)), dma((ny,)),
-            dma((nx,)), dma((nx,)), dma((nc,)), dma((nc,)),
+            dma((nc,)), dma((nc,)), dma((nx,)), dma((nx,)),
             dma((ny,)), dma((ny,)), dma((nz,)), dma((nz,)),
+            dma((ny,)), dma((ny,)), dma((nx,)), dma((nx,)),
+            dma((nc,)), dma((nc,)),
         ],
         compiler_params=pltpu.CompilerParams(collective_id=0, has_side_effects=True),
     )(tiles)

time: 156 us -> 142 us (0.910)
  Pallas kernels: 86.6 us -> 72.6 us
    pallas_call x1, Pallas kernels: 58.5 us -> 44.5 us  [all_sum(): pl.pallas_call(functools.partial(sum_kernel, sizes), out_shape=jax.ShapeD...]
where the time goes in v4:
time: 142 us
  Pallas kernels  72.6 us (51%)
  other arithmetic  53.8 us (38%)
  local copies, waits for them, and re-layouts  9.41 us (7%)
  matrix products  3.7 us (3%)
  between operations  2.09 us (1%)
    pallas_call x1, Pallas kernels, all_sum(): pl.pallas_call(functools.partial(sum_kernel, sizes), out_shape=jax.ShapeD...  44.5 us
    another operation x6, other arithmetic, shards(): lower = jnp.linalg.cholesky(gram)  34.1 us
    pallas_call x1, Pallas kernels, sketch_scatter(): pl.pallas_call(functools.partial(scatter_kernel, nx), out_shape=jax.Shape...  28.1 us
    another operation x2, other arithmetic, shards(): lax.linalg.triangular_solve(lower, rotation, left_side=True, lower=True,...  19.7 us
    another operation x6, local copies, waits for them, and re-layouts  4.06 us
    unnamed x7, local copies, waits for them, and re-layouts  3.38 us

profile of v4, /device:TPU:1, one launch (start us, length us, event | category | flops | bytes accessed | tf_op | source)
XLA Modules:
  0.0 141.7 jit_solution(15032251781982612077)
XLA Ops:
  0.6 0.0 copy-start
  0.6 1.6 %copy-done = bf16[2048,512]{1,0:T(8,128)(2,1)S(1)} copy-done((bf16[2048,512]{1,0:T(8,128)(2,1)S(1)}, bf16[2048,512]{1,0:T(8,128)(2,1)}, u32[]{:S(2)}) %copy-start) | copy-done | bytes 2097176
  2.2 0.0 copy-start.1
  2.2 0.9 copy-done.1
  3.2 28.1 %shard_map.50 = f32[512,256]{1,0:T(8,128)S(1)} custom-call(bf16[2048,512]{1,0:T(8,128)(2,1)S(1)} %copy-done, bf16[512,256]{1,0:T(8,128)(2,1)S(1)} %copy-done.1), custom_call_target="tpu_custom_call" | custom-call | tf_op jit(solution)/shard_map/pallas_call | solution.py:165
  31.3 1.0 fusion.14
  32.3 0.7 reshape.27.a_ref
  33.0 44.5 %shard_map.51 = f32[64,8,128]{2,1,0:T(8,128)} custom-call(f32[64,8,128]{2,1,0:T(8,128)} %reshape.27.a_ref), custom_call_target="tpu_custom_call" | custom-call | tf_op jit(solution)/shard_map/pallas_call | solution.py:101
  77.6 1.0 reshape.28
  78.6 0.0 copy-start.2
  78.6 0.1 copy.7
  78.8 11.7 %cholesky.50 = f32[128,128]{1,0:T(8,128)S(1)} custom-call(f32[128,128]{1,0:T(8,128)S(1)} %cholesky.118), custom_call_target="Cholesky" | custom-call | tf_op jit(solution)/shard_map/jit(cholesky)/cholesky | solution.py:190
  90.5 9.8 %custom-call.14 = f32[1,128,128]{1,2,0:T(8,128)S(1)} custom-call(f32[1,128,128]{2,1,0:T(8,128)S(1)} %get-tuple-element.29), custom_call_target="InvertDiagBlocksLowerTriangular" | custom-call | tf_op jit(solution)/shard_map/jit(cholesky)/cholesky | solution.py:190
  100.4 0.2 constant_dynamic-update-slice_fusion.1
  100.6 0.3 convolution_subtract_fusion.1
  100.9 11.8 %cholesky.105 = f32[128,128]{1,0:T(8,128)S(1)} custom-call(f32[128,128]{1,0:T(8,128)S(1)} %convolution_subtract_fusion.1), custom_call_target="Cholesky" | custom-call | tf_op jit(solution)/shard_map/jit(cholesky)/cholesky | solution.py:190
  112.7 0.6 compare_reduce_fusion
  114.8 0.1 triangular_solve.57
  114.8 4.1 %while.1 = (s32[]{:T(128)}, f32[256,256]{1,0:T(8,128)S(1)}, s32[2,2]{1,0:T(2,128)S(1)}, f32[2,128,128]{2,1,0:T(8,128)S(1)}, s32[]{:T(128)}) while((s32[]{:T(128)}, f32[256,256]{1,0:T(8,128)S(1)}, s32[2,2]{1,0:T(2,128)S(1)}, f32[2,128,128]{2,1,0:T(8,128)S(1)}, s32[]{:T(128)}) %tuple.30), condition=%wide.while_cond, body=%wide.while_body.sunk | while | flops 2 | bytes 131181 | solution.py:191
  114.8 0.6 fusion.23
  115.4 1.4 %bitcast_dynamic-update-slice_fusion.2 = f32[2,128,128]{2,1,0:T(8,128)S(1)} fusion(f32[2,128,128]{2,1,0:T(8,128)S(1)} %get-tuple-element.71, s32[]{:T(128)} %get-tuple-element.68, f32[256,256]{1,0:T(8,128)S(1)} %get-tuple-element.74, s32[]{:T(128)} %bitcast.34, s32[]{:T(128)} %bitcast.35), kind=kLoop, calls=%fused_computation.clone.1 | loop fusion | bytes 131084 | tf_op jit(solution)/shard_map/triangular_solve
  116.9 0.6 fusion.23
  117.5 1.4 %bitcast_dynamic-update-slice_fusion.2 = f32[2,128,128]{2,1,0:T(8,128)S(1)} fusion(f32[2,128,128]{2,1,0:T(8,128)S(1)} %get-tuple-element.71, s32[]{:T(128)} %get-tuple-element.68, f32[256,256]{1,0:T(8,128)S(1)} %get-tuple-element.74, s32[]{:T(128)} %bitcast.34, s32[]{:T(128)} %bitcast.35), kind=kLoop, calls=%fused_computation.clone.1 | loop fusion | bytes 131084 | tf_op jit(solution)/shard_map/triangular_solve
  118.9 19.7 %custom-call.15 = f32[2,128,128]{1,2,0:T(8,128)S(1)} custom-call(f32[2,128,128]{2,1,0:T(8,128)S(1)} %get-tuple-element.9), custom_call_target="InvertDiagBlocksLowerTriangular" | custom-call | tf_op jit(solution)/shard_map/triangular_solve | solution.py:191
  138.6 0.0 copy-done.2
  138.6 0.3 fusion.5
  138.9 0.3 convolution_subtract_fusion
  139.2 0.3 fusion.8
  139.5 1.4 convolution_multiply_fusion
  140.9 0.8 copy.8
  (10 shorter events, 0.2 us)
Async XLA Ops:
  0.6 1.6 %copy-start = (bf16[2048,512]{1,0:T(8,128)(2,1)S(1)}, bf16[2048,512]{1,0:T(8,128)(2,1)}, u32[]{:S(2)}) copy-start(bf16[2048,512]{1,0:T(8,128)(2,1)} %s_ref.1) | copy-start | bytes 6291460
  2.2 0.9 copy-start.1
  78.6 60.0 %copy-start.2 = (f32[256,256]{1,0:T(8,128)S(1)}, f32[256,256]{1,0:T(8,128)}, u32[]{:S(2)}) copy-start(f32[256,256]{1,0:T(8,128)} %param.5) | copy-start | bytes 786436

commit v5 on v4

--- a/solution.py
+++ b/solution.py
@@ -177,6 +177,58 @@
     )(snapshots, sketch)
 
 
+def factor_kernel(b, g_ref, l_ref, w_ref):
+    n = g_ref.shape[0]
+    hi = lax.Precision.HIGHEST
+    l_ref[...] = jnp.zeros_like(l_ref)
+    w_ref[...] = jnp.zeros_like(w_ref)
+    nt = (((1,), (1,)), ((), ()))
+    rows = lax.broadcasted_iota(jnp.int32, (b, b), 0)
+    cols = lax.broadcasted_iota(jnp.int32, (b, b), 1)
+
+    def panel(p, carry):
+        r0 = pl.multiple_of(p * b, b)
+        arow = g_ref[pl.ds(r0, b), :]
+        w = w_ref[...]
+        x = lax.dot_general(arow, w, nt, precision=hi, preferred_element_type=jnp.float32)
+        pick = (lax.broadcasted_iota(jnp.int32, (n, b), 0)
+                == r0 + lax.broadcasted_iota(jnp.int32, (n, b), 1)).astype(jnp.float32)
+        place = (lax.broadcasted_iota(jnp.int32, (b, n), 1)
+                 == r0 + lax.broadcasted_iota(jnp.int32, (b, n), 0)).astype(jnp.float32)
+        s = jnp.dot(arow, pick, precision=hi, preferred_element_type=jnp.float32)
+        s = s - lax.dot_general(x, x, nt, precision=hi, preferred_element_type=jnp.float32)
+        low = jnp.zeros((b, b), jnp.float32)
+        inv = jnp.zeros((b, b), jnp.float32)
+        rest = (rows == cols).astype(jnp.float32)
+        for i in range(b):
+            root = jnp.sqrt(s[i:i + 1, i:i + 1])
+            col = jnp.where(rows[:, i:i + 1] >= i, s[:, i:i + 1] / root, 0.0)
+            row = jnp.where(cols[i:i + 1, :] >= i, s[i:i + 1, :] / root, 0.0)
+            s = s - col * row
+            low = jnp.where(cols == i, col, low)
+            irow = rest[i:i + 1, :] / col[i:i + 1, :]
+            inv = jnp.where(rows == i, irow, inv)
+            rest = rest - col * irow
+        l_ref[pl.ds(r0, b), :] = x + jnp.dot(low, place, precision=hi,
+                                             preferred_element_type=jnp.float32)
+        y = jnp.dot(x, w, precision=hi, preferred_element_type=jnp.float32)
+        w_ref[pl.ds(r0, b), :] = jnp.dot(inv, place - y, precision=hi,
+                                         preferred_element_type=jnp.float32)
+        return carry
+
+    lax.fori_loop(0, n // b, panel, 0)
+
+
+def factor(gram, b=32):
+    n = gram.shape[0]
+    return pl.pallas_call(
+        functools.partial(factor_kernel, b),
+        out_shape=(jax.ShapeDtypeStruct((n, n), jnp.float32),) * 2,
+        in_specs=[pl.BlockSpec(memory_space=pltpu.VMEM)],
+        out_specs=(pl.BlockSpec(memory_space=pltpu.VMEM),) * 2,
+    )(gram)
+
+
 def shards(sizes, snapshots, sketch, rotation):
     sketched = sketch_scatter(snapshots, sketch, sizes[3])
     gram = lax.dot_general(
@@ -187,9 +239,10 @@
         preferred_element_type=jnp.float32,
     )
     gram = all_sum(gram, sizes)
-    lower = jnp.linalg.cholesky(gram)
-    rotated = lax.linalg.triangular_solve(
-        lower, rotation, left_side=True, lower=True, transpose_a=True
+    lower, inverse = factor(gram)
+    rotated = lax.dot_general(
+        inverse, rotation, (((0,), (0,)), ((), ())),
+        precision=lax.Precision.HIGHEST, preferred_element_type=jnp.float32,
     )
     cell_count = sketched.shape[0] * sizes[0] * sizes[1] * sizes[2] * sizes[3]
     scale = jnp.sqrt(jnp.float32(cell_count))

time: 142 us -> 119 us (0.84)
  other arithmetic: 53.8 us -> 0.02 us
  Pallas kernels: 72.6 us -> 108 us
  local copies, waits for them, and re-layouts: 9.41 us -> 5.87 us
    another operation x8 -> x0, other arithmetic: 53.8 us -> none  [the longest x6 34.1 us: shards(): lower = jnp.linalg.cholesky(gram)]
    pallas_call x0 -> x1, Pallas kernels: none -> 35.4 us  [factor(): pl.pallas_call(functools.partial(factor_kernel, b), out_shape=(jax.ShapeD...]
    another operation x9 -> x0, local copies, waits for them, and re-layouts: 4.16 us -> none
    dot_general x0 -> x1, matrix products: none -> 1.59 us  [shards(): lax.dot_general(inverse, rotation, (((0,), (0,)), ((), ())), precision=la...]
    unnamed x7 -> x9, local copies, waits for them, and re-layouts: 3.38 us -> 3.43 us
where the time goes in v5:
time: 119 us
  Pallas kernels  108 us (91%)
  local copies, waits for them, and re-layouts  5.87 us (5%)
  matrix products  3.98 us (3%)
    pallas_call x1, Pallas kernels, all_sum(): pl.pallas_call(functools.partial(sum_kernel, sizes), out_shape=jax.ShapeD...  44.5 us
    pallas_call x1, Pallas kernels, factor(): pl.pallas_call(functools.partial(factor_kernel, b), out_shape=(jax.ShapeD...  35.4 us
    pallas_call x1, Pallas kernels, sketch_scatter(): pl.pallas_call(functools.partial(scatter_kernel, nx), out_shape=jax.Shape...  28.1 us
    unnamed x9, local copies, waits for them, and re-layouts  3.43 us

profile of v5, /device:TPU:1, one launch (start us, length us, event | category | flops | bytes accessed | tf_op | source)
XLA Modules:
  0.0 118.6 jit_solution(17789129320257039008)
XLA Ops:
  0.6 0.0 copy-start
  0.6 0.0 copy-start.1
  0.7 1.6 %copy-done.1 = bf16[2048,512]{1,0:T(8,128)(2,1)S(1)} copy-done((bf16[2048,512]{1,0:T(8,128)(2,1)S(1)}, bf16[2048,512]{1,0:T(8,128)(2,1)}, u32[]{:S(2)}) %copy-start.1) | copy-done | bytes 2097176
  2.3 0.0 copy-start.2
  2.3 0.9 copy-done.2
  3.2 28.1 %shard_map.50 = f32[512,256]{1,0:T(8,128)S(1)} custom-call(bf16[2048,512]{1,0:T(8,128)(2,1)S(1)} %copy-done.1, bf16[512,256]{1,0:T(8,128)(2,1)S(1)} %copy-done.2), custom_call_target="tpu_custom_call" | custom-call | tf_op jit(solution)/shard_map/pallas_call | solution.py:165
  31.4 1.0 fusion
  32.4 0.7 reshape.10.a_ref
  33.1 44.5 %shard_map.51 = f32[64,8,128]{2,1,0:T(8,128)} custom-call(f32[64,8,128]{2,1,0:T(8,128)} %reshape.10.a_ref), custom_call_target="tpu_custom_call" | custom-call | tf_op jit(solution)/shard_map/pallas_call | solution.py:101
  77.6 1.7 %reshape.11.g_ref = f32[256,256]{1,0:T(8,128)} reshape(f32[64,8,128]{2,1,0:T(8,128)} %shard_map.51) | data formatting | bytes 524288 | tf_op jit(solution)/shard_map/reshape | solution.py:122
  79.3 35.4 %shard_map.52 = (f32[256,256]{1,0:T(8,128)}, f32[256,256]{1,0:T(8,128)}) custom-call(f32[256,256]{1,0:T(8,128)} %reshape.11.g_ref), custom_call_target="tpu_custom_call" | custom-call | tf_op jit(solution)/shard_map/pallas_call | solution.py:224
  114.8 0.0 copy-start.3
  114.8 0.0 copy-done
  114.8 1.6 %fusion.1 = f32[256,256]{1,0:T(8,128)S(1)} fusion(f32[256,256]{1,0:T(8,128)} %get-tuple-element.4, f32[256,256]{1,0:T(8,128)S(1)} %copy-done), kind=kOutput, calls=%fused_computation.3 | convolution fusion | flops 201326592 | bytes 786432 | tf_op jit(solution)/shard_map/dot_general | solution.py:243
  116.4 1.4 %convolution_multiply_fusion = f32[512,256]{1,0:T(8,128)} fusion(f32[512,256]{1,0:T(8,128)S(1)} %shard_map.50, f32[256,256]{1,0:T(8,128)S(1)} %fusion.1), kind=kOutput, calls=%fused_computation | convolution fusion | flops 402784256 | bytes 1310720 | tf_op jit(solution)/shard_map/dot_general | solution.py:249
  117.7 0.0 copy-done.3
  117.8 0.8 copy.5
  (1 shorter events, 0.0 us)
Async XLA Ops:
  0.6 114.1 %copy-start = (f32[256,256]{1,0:T(8,128)S(1)}, f32[256,256]{1,0:T(8,128)}, u32[]{:S(2)}) copy-start(f32[256,256]{1,0:T(8,128)} %param.5) | copy-start | bytes 786436
  0.6 1.6 %copy-start.1 = (bf16[2048,512]{1,0:T(8,128)(2,1)S(1)}, bf16[2048,512]{1,0:T(8,128)(2,1)}, u32[]{:S(2)}) copy-start(bf16[2048,512]{1,0:T(8,128)(2,1)} %s_ref.1) | copy-start | bytes 6291460
  2.3 0.9 copy-start.2
  114.8 3.0 %copy-start.3 = (f32[256,256]{1,0:T(8,128)S(1)}, f32[256,256]{1,0:T(8,128)}, u32[]{:S(2)}) copy-start(f32[256,256]{1,0:T(8,128)} %get-tuple-element.5) | copy-start | bytes 786436

commit v6 on v5

--- a/solution.py
+++ b/solution.py
@@ -10,7 +10,6 @@
 MESH = pl.DeviceIdType.MESH
 AXES = ("z", "y", "c", "x")
 SPACE = ("z", "y", "c")
-TILES = 64
 
 
 def sum_kernel(sizes, a_ref, o_ref, cbuf, csum, xbuf, xsum, ybuf, ysum, zbuf, full,
@@ -55,7 +54,7 @@
             acc = acc + buf[j]
         return acc
 
-    c1 = TILES // nc
+    c1 = a_ref.shape[0] // nc
     c2 = c1 // nx
     c3 = c2 // ny
     zdev = lambda j: (j, yi, ci, xi)
@@ -91,16 +90,14 @@
 
 def all_sum(gram, sizes):
     nz, ny, nc, nx = sizes
-    c1 = TILES // nc
+    c1 = gram.shape[0] // nc
     c2 = c1 // nx
     c3 = c2 // ny
-    rows, cols = gram.shape
-    tiles = gram.reshape(TILES, (rows * cols) // (TILES * 128), 128)
-    t = tiles.shape[1:]
+    t = gram.shape[1:]
     dma = pltpu.SemaphoreType.DMA
-    out = pl.pallas_call(
+    return pl.pallas_call(
         functools.partial(sum_kernel, sizes),
-        out_shape=jax.ShapeDtypeStruct(tiles.shape, jnp.float32),
+        out_shape=jax.ShapeDtypeStruct(gram.shape, jnp.float32),
         in_specs=[pl.BlockSpec(memory_space=pltpu.VMEM)],
         out_specs=pl.BlockSpec(memory_space=pltpu.VMEM),
         scratch_shapes=[
@@ -111,15 +108,14 @@
             pltpu.VMEM((ny, c3) + t, jnp.float32),
             pltpu.VMEM((c3,) + t, jnp.float32),
             pltpu.VMEM((nz, c3) + t, jnp.float32),
-            pltpu.VMEM(tiles.shape, jnp.float32),
+            pltpu.VMEM(gram.shape, jnp.float32),
             dma((nc,)), dma((nc,)), dma((nx,)), dma((nx,)),
             dma((ny,)), dma((ny,)), dma((nz,)), dma((nz,)),
             dma((ny,)), dma((ny,)), dma((nx,)), dma((nx,)),
             dma((nc,)), dma((nc,)),
         ],
         compiler_params=pltpu.CompilerParams(collective_id=0, has_side_effects=True),
-    )(tiles)
-    return out.reshape(rows, cols)
+    )(gram)
 
 
 def scatter_kernel(nx, s_ref, k_ref, o_ref, part, rbuf, rs, ss):
@@ -219,7 +215,7 @@
     lax.fori_loop(0, n // b, panel, 0)
 
 
-def factor(gram, b=32):
+def factor(gram, b=64):
     n = gram.shape[0]
     return pl.pallas_call(
         functools.partial(factor_kernel, b),

time: 119 us -> 114 us (0.958)
  Pallas kernels: 108 us -> 105 us
  local copies, waits for them, and re-layouts: 5.87 us -> 3.43 us
    pallas_call x1, Pallas kernels: 35.4 us -> 32 us  [factor(): pl.pallas_call(functools.partial(factor_kernel, b), out_shape=(jax.ShapeD...]
    reshape x2 -> x0, local copies, waits for them, and re-layouts: 2.45 us -> none  [the longest x1 1.73 us: all_sum(): return out.reshape(rows, cols)]
where the time goes in v6:
time: 114 us; the launch traced here: 113 us
  Pallas kernels  105 us (92%)
  matrix products  4.69 us (4%)
  local copies, waits for them, and re-layouts  3.43 us (3%)
    pallas_call x1, Pallas kernels, all_sum(): pl.pallas_call(functools.partial(sum_kernel, sizes), out_shape=jax.ShapeD...  44.5 us
    pallas_call x1, Pallas kernels, factor(): pl.pallas_call(functools.partial(factor_kernel, b), out_shape=(jax.ShapeD...  32 us
    pallas_call x1, Pallas kernels, sketch_scatter(): pl.pallas_call(functools.partial(scatter_kernel, nx), out_shape=jax.Shape...  28.1 us
    unnamed x9, local copies, waits for them, and re-layouts  3.43 us

profile of v6, /device:TPU:1, one launch (start us, length us, event | category | flops | bytes accessed | tf_op | source)
XLA Modules:
  0.0 113.4 jit_solution(1502314497676618567)
XLA Ops:
  0.6 0.0 copy-start
  0.6 0.0 copy-start.1
  0.7 1.6 %copy-done.1 = bf16[2048,512]{1,0:T(8,128)(2,1)S(1)} copy-done((bf16[2048,512]{1,0:T(8,128)(2,1)S(1)}, bf16[2048,512]{1,0:T(8,128)(2,1)}, u32[]{:S(2)}) %copy-start.1) | copy-done | bytes 2097176
  2.3 0.0 copy-start.2
  2.3 0.9 copy-done.2
  3.2 28.1 %shard_map.50 = f32[512,256]{1,0:T(8,128)S(1)} custom-call(bf16[2048,512]{1,0:T(8,128)(2,1)S(1)} %copy-done.1, bf16[512,256]{1,0:T(8,128)(2,1)S(1)} %copy-done.2), custom_call_target="tpu_custom_call" | custom-call | tf_op jit(solution)/shard_map/pallas_call | solution.py:161
  31.4 1.7 %fusion.a_ref = f32[256,256]{1,0:T(8,128)} fusion(f32[512,256]{1,0:T(8,128)S(1)} %shard_map.50), kind=kOutput, calls=%fused_computation.2 | convolution fusion | flops 402653184 | bytes 786432 | tf_op jit(solution)/shard_map/dot_general | solution.py:230
  33.1 44.5 %shard_map.51.g_ref = f32[256,256]{1,0:T(8,128)} custom-call(f32[256,256]{1,0:T(8,128)} %fusion.a_ref), custom_call_target="tpu_custom_call" | custom-call | tf_op jit(solution)/shard_map/pallas_call | solution.py:98
  77.6 32.0 %shard_map.52 = (f32[256,256]{1,0:T(8,128)}, f32[256,256]{1,0:T(8,128)}) custom-call(f32[256,256]{1,0:T(8,128)} %shard_map.51.g_ref), custom_call_target="tpu_custom_call" | custom-call | tf_op jit(solution)/shard_map/pallas_call | solution.py:220
  109.6 0.0 copy-start.3
  109.6 0.0 copy-done
  109.6 1.6 %fusion.1 = f32[256,256]{1,0:T(8,128)S(1)} fusion(f32[256,256]{1,0:T(8,128)} %get-tuple-element.4, f32[256,256]{1,0:T(8,128)S(1)} %copy-done), kind=kOutput, calls=%fused_computation.3 | convolution fusion | flops 201326592 | bytes 786432 | tf_op jit(solution)/shard_map/dot_general | solution.py:239
  111.2 1.4 %convolution_multiply_fusion = f32[512,256]{1,0:T(8,128)} fusion(f32[512,256]{1,0:T(8,128)S(1)} %shard_map.50, f32[256,256]{1,0:T(8,128)S(1)} %fusion.1), kind=kOutput, calls=%fused_computation | convolution fusion | flops 402784256 | bytes 1310720 | tf_op jit(solution)/shard_map/dot_general | solution.py:245
  112.6 0.0 copy-done.3
  112.6 0.8 copy.5
  (1 shorter events, 0.0 us)
Async XLA Ops:
  0.6 109.0 %copy-start = (f32[256,256]{1,0:T(8,128)S(1)}, f32[256,256]{1,0:T(8,128)}, u32[]{:S(2)}) copy-start(f32[256,256]{1,0:T(8,128)} %param.5) | copy-start | bytes 786436
  0.6 1.6 %copy-start.1 = (bf16[2048,512]{1,0:T(8,128)(2,1)S(1)}, bf16[2048,512]{1,0:T(8,128)(2,1)}, u32[]{:S(2)}) copy-start(bf16[2048,512]{1,0:T(8,128)(2,1)} %s_ref.1) | copy-start | bytes 6291460
  2.3 0.9 copy-start.2
  109.6 3.0 %copy-start.3 = (f32[256,256]{1,0:T(8,128)S(1)}, f32[256,256]{1,0:T(8,128)}, u32[]{:S(2)}) copy-start(f32[256,256]{1,0:T(8,128)} %get-tuple-element.5) | copy-start | bytes 786436

commit v7 on v6

--- a/solution.py
+++ b/solution.py
@@ -197,10 +197,10 @@
         inv = jnp.zeros((b, b), jnp.float32)
         rest = (rows == cols).astype(jnp.float32)
         for i in range(b):
-            root = jnp.sqrt(s[i:i + 1, i:i + 1])
-            col = jnp.where(rows[:, i:i + 1] >= i, s[:, i:i + 1] / root, 0.0)
-            row = jnp.where(cols[i:i + 1, :] >= i, s[i:i + 1, :] / root, 0.0)
-            s = s - col * row
+            pivot = s[i:i + 1, i:i + 1]
+            left = s[:, i:i + 1]
+            s = s - left * (s[i:i + 1, :] * (1.0 / pivot))
+            col = jnp.where(rows[:, i:i + 1] >= i, left / jnp.sqrt(pivot), 0.0)
             low = jnp.where(cols == i, col, low)
             irow = rest[i:i + 1, :] / col[i:i + 1, :]
             inv = jnp.where(rows == i, irow, inv)
@@ -215,7 +215,7 @@
     lax.fori_loop(0, n // b, panel, 0)
 
 
-def factor(gram, b=64):
+def factor(gram, b=128):
     n = gram.shape[0]
     return pl.pallas_call(
         functools.partial(factor_kernel, b),

time: 114 us -> 108 us (0.947)
  Pallas kernels: 105 us -> 98.8 us
    pallas_call x1, Pallas kernels: 32 us -> 26.2 us  [factor(): pl.pallas_call(functools.partial(factor_kernel, b), out_shape=(jax.ShapeD...]
where the time goes in v7:
time: 108 us
  Pallas kernels  98.8 us (91%)
  matrix products  4.69 us (4%)
  local copies, waits for them, and re-layouts  3.43 us (3%)
    pallas_call x1, Pallas kernels, all_sum(): pl.pallas_call(functools.partial(sum_kernel, sizes), out_shape=jax.ShapeD...  44.5 us
    pallas_call x1, Pallas kernels, sketch_scatter(): pl.pallas_call(functools.partial(scatter_kernel, nx), out_shape=jax.Shape...  28.1 us
    pallas_call x1, Pallas kernels, factor(): pl.pallas_call(functools.partial(factor_kernel, b), out_shape=(jax.ShapeD...  26.2 us
    unnamed x9, local copies, waits for them, and re-layouts  3.43 us

profile of v7, /device:TPU:1, one launch (start us, length us, event | category | flops | bytes accessed | tf_op | source)
XLA Modules:
  0.0 107.7 jit_solution(12870106647156978424)
XLA Ops:
  0.6 0.0 copy-start
  0.6 0.0 copy-start.1
  0.7 1.6 %copy-done.1 = bf16[2048,512]{1,0:T(8,128)(2,1)S(1)} copy-done((bf16[2048,512]{1,0:T(8,128)(2,1)S(1)}, bf16[2048,512]{1,0:T(8,128)(2,1)}, u32[]{:S(2)}) %copy-start.1) | copy-done | bytes 2097176
  2.3 0.0 copy-start.2
  2.3 0.9 copy-done.2
  3.2 28.1 %shard_map.50 = f32[512,256]{1,0:T(8,128)S(1)} custom-call(bf16[2048,512]{1,0:T(8,128)(2,1)S(1)} %copy-done.1, bf16[512,256]{1,0:T(8,128)(2,1)S(1)} %copy-done.2), custom_call_target="tpu_custom_call" | custom-call | tf_op jit(solution)/shard_map/pallas_call | solution.py:161
  31.4 1.7 %fusion.a_ref = f32[256,256]{1,0:T(8,128)} fusion(f32[512,256]{1,0:T(8,128)S(1)} %shard_map.50), kind=kOutput, calls=%fused_computation.2 | convolution fusion | flops 402653184 | bytes 786432 | tf_op jit(solution)/shard_map/dot_general | solution.py:230
  33.1 44.5 %shard_map.51.g_ref = f32[256,256]{1,0:T(8,128)} custom-call(f32[256,256]{1,0:T(8,128)} %fusion.a_ref), custom_call_target="tpu_custom_call" | custom-call | tf_op jit(solution)/shard_map/pallas_call | solution.py:98
  77.6 26.2 %shard_map.52 = (f32[256,256]{1,0:T(8,128)}, f32[256,256]{1,0:T(8,128)}) custom-call(f32[256,256]{1,0:T(8,128)} %shard_map.51.g_ref), custom_call_target="tpu_custom_call" | custom-call | tf_op jit(solution)/shard_map/pallas_call | solution.py:220
  103.8 0.0 copy-start.3
  103.8 0.0 copy-done
  103.8 1.6 %fusion.1 = f32[256,256]{1,0:T(8,128)S(1)} fusion(f32[256,256]{1,0:T(8,128)} %get-tuple-element.4, f32[256,256]{1,0:T(8,128)S(1)} %copy-done), kind=kOutput, calls=%fused_computation.3 | convolution fusion | flops 201326592 | bytes 786432 | tf_op jit(solution)/shard_map/dot_general | solution.py:239
  105.4 1.4 %convolution_multiply_fusion = f32[512,256]{1,0:T(8,128)} fusion(f32[512,256]{1,0:T(8,128)S(1)} %shard_map.50, f32[256,256]{1,0:T(8,128)S(1)} %fusion.1), kind=kOutput, calls=%fused_computation | convolution fusion | flops 402784256 | bytes 1310720 | tf_op jit(solution)/shard_map/dot_general | solution.py:245
  106.8 0.0 copy-done.3
  106.8 0.8 copy.5
  (1 shorter events, 0.0 us)
Async XLA Ops:
  0.6 103.2 %copy-start = (f32[256,256]{1,0:T(8,128)S(1)}, f32[256,256]{1,0:T(8,128)}, u32[]{:S(2)}) copy-start(f32[256,256]{1,0:T(8,128)} %param.5) | copy-start | bytes 786436
  0.6 1.6 %copy-start.1 = (bf16[2048,512]{1,0:T(8,128)(2,1)S(1)}, bf16[2048,512]{1,0:T(8,128)(2,1)}, u32[]{:S(2)}) copy-start(bf16[2048,512]{1,0:T(8,128)(2,1)} %s_ref.1) | copy-start | bytes 6291460
  2.3 0.9 copy-start.2
  103.8 3.0 %copy-start.3 = (f32[256,256]{1,0:T(8,128)S(1)}, f32[256,256]{1,0:T(8,128)}, u32[]{:S(2)}) copy-start(f32[256,256]{1,0:T(8,128)} %get-tuple-element.5) | copy-start | bytes 786436

commit v8 on v7

--- a/solution.py
+++ b/solution.py
@@ -12,22 +12,23 @@
 SPACE = ("z", "y", "c")
 
 
-def sum_kernel(sizes, a_ref, o_ref, cbuf, csum, xbuf, xsum, ybuf, ysum, zbuf, full,
-               cr, cs, xr, xs, yr, ys, zr, zs, ygr, ygs, xgr, xgs, cgr, cgs):
+def sum_kernel(sizes, a_ref, o_ref, cbuf, csum, qbuf, qsum, zbuf, full,
+               cr, cs, qr, qs, zr, zs, qgr, qgs, cgr, cgs):
     nz, ny, nc, nx = sizes
+    nq = nx * ny
     zi, yi, ci, xi = (lax.axis_index(a) for a in AXES)
+    qi = xi * ny + yi
 
     def peers(n, me):
         return [lax.rem(me + d, n) for d in range(1, n)]
 
+    zdev = lambda j: (j, yi, ci, xi)
+    cdev = lambda j: (zi, yi, j, xi)
+    qdev = lambda q: (zi, lax.rem(q, ny), ci, q // ny)
+
     barrier = pltpu.get_barrier_semaphore()
     count = 0
-    for n, me, make in (
-        (nz, zi, lambda j: (j, yi, ci, xi)),
-        (ny, yi, lambda j: (zi, j, ci, xi)),
-        (nc, ci, lambda j: (zi, yi, j, xi)),
-        (nx, xi, lambda j: (zi, yi, ci, j)),
-    ):
+    for n, me, make in ((nz, zi, zdev), (nq, qi, qdev), (nc, ci, cdev)):
         for j in peers(n, me):
             pl.semaphore_signal(barrier, inc=1, device_id=make(j), device_id_type=MESH)
             count += 1
@@ -55,34 +56,23 @@
         return acc
 
     c1 = a_ref.shape[0] // nc
-    c2 = c1 // nx
-    c3 = c2 // ny
-    zdev = lambda j: (j, yi, ci, xi)
-    ydev = lambda j: (zi, j, ci, xi)
-    cdev = lambda j: (zi, yi, j, xi)
-    xdev = lambda j: (zi, yi, ci, j)
+    c2 = c1 // nq
 
     cbuf[ci] = a_ref[pl.ds(ci * c1, c1)]
     exchange(nc, ci, cdev, lambda j: a_ref.at[pl.ds(j * c1, c1)], lambda j: cbuf.at[j], cr, cs)
     csum[...] = ordered_sum(cbuf, nc)
 
-    xbuf[xi] = csum[pl.ds(xi * c2, c2)]
-    exchange(nx, xi, xdev, lambda j: csum.at[pl.ds(j * c2, c2)], lambda j: xbuf.at[j], xr, xs)
-    xsum[...] = ordered_sum(xbuf, nx)
-
-    ybuf[yi] = xsum[pl.ds(yi * c3, c3)]
-    exchange(ny, yi, ydev, lambda j: xsum.at[pl.ds(j * c3, c3)], lambda j: ybuf.at[j], yr, ys)
-    ysum[...] = ordered_sum(ybuf, ny)
-
-    zbuf[zi] = ysum[...]
-    exchange(nz, zi, zdev, lambda j: ysum, lambda j: zbuf.at[j], zr, zs)
-    own = ci * c1 + xi * c2 + yi * c3
-    full[pl.ds(own, c3)] = ordered_sum(zbuf, nz)
-
-    exchange(ny, yi, ydev, lambda j: full.at[pl.ds(own, c3)],
-             lambda j: full.at[pl.ds(ci * c1 + xi * c2 + j * c3, c3)], ygr, ygs)
-    exchange(nx, xi, xdev, lambda j: full.at[pl.ds(ci * c1 + xi * c2, c2)],
-             lambda j: full.at[pl.ds(ci * c1 + j * c2, c2)], xgr, xgs)
+    qbuf[qi] = csum[pl.ds(qi * c2, c2)]
+    exchange(nq, qi, qdev, lambda j: csum.at[pl.ds(j * c2, c2)], lambda j: qbuf.at[j], qr, qs)
+    qsum[...] = ordered_sum(qbuf, nq)
+
+    zbuf[zi] = qsum[...]
+    exchange(nz, zi, zdev, lambda j: qsum, lambda j: zbuf.at[j], zr, zs)
+    own = ci * c1 + qi * c2
+    full[pl.ds(own, c2)] = ordered_sum(zbuf, nz)
+
+    exchange(nq, qi, qdev, lambda j: full.at[pl.ds(own, c2)],
+             lambda j: full.at[pl.ds(ci * c1 + j * c2, c2)], qgr, qgs)
     exchange(nc, ci, cdev, lambda j: full.at[pl.ds(ci * c1, c1)],
              lambda j: full.at[pl.ds(j * c1, c1)], cgr, cgs)
     o_ref[...] = full[...]
@@ -90,9 +80,9 @@
 
 def all_sum(gram, sizes):
     nz, ny, nc, nx = sizes
+    nq = nx * ny
     c1 = gram.shape[0] // nc
-    c2 = c1 // nx
-    c3 = c2 // ny
+    c2 = c1 // nq
     t = gram.shape[1:]
     dma = pltpu.SemaphoreType.DMA
     return pl.pallas_call(
@@ -103,15 +93,12 @@
         scratch_shapes=[
             pltpu.VMEM((nc, c1) + t, jnp.float32),
             pltpu.VMEM((c1,) + t, jnp.float32),
-            pltpu.VMEM((nx, c2) + t, jnp.float32),
+            pltpu.VMEM((nq, c2) + t, jnp.float32),
             pltpu.VMEM((c2,) + t, jnp.float32),
-            pltpu.VMEM((ny, c3) + t, jnp.float32),
-            pltpu.VMEM((c3,) + t, jnp.float32),
-            pltpu.VMEM((nz, c3) + t, jnp.float32),
+            pltpu.VMEM((nz, c2) + t, jnp.float32),
             pltpu.VMEM(gram.shape, jnp.float32),
-            dma((nc,)), dma((nc,)), dma((nx,)), dma((nx,)),
-            dma((ny,)), dma((ny,)), dma((nz,)), dma((nz,)),
-            dma((ny,)), dma((ny,)), dma((nx,)), dma((nx,)),
+            dma((nc,)), dma((nc,)), dma((nq,)), dma((nq,)),
+            dma((nz,)), dma((nz,)), dma((nq,)), dma((nq,)),
             dma((nc,)), dma((nc,)),
         ],
         compiler_params=pltpu.CompilerParams(collective_id=0, has_side_effects=True),

time: 108 us -> 104 us (0.963)
  Pallas kernels: 98.8 us -> 94.7 us
    pallas_call x1, Pallas kernels: 44.5 us -> 40.4 us  [all_sum(): pl.pallas_call(functools.partial(sum_kernel, sizes), out_shape=jax.ShapeD...]
where the time goes in v8:
time: 104 us
  Pallas kernels  94.7 us (91%)
  matrix products  4.69 us (5%)
  local copies, waits for them, and re-layouts  3.43 us (3%)
    pallas_call x1, Pallas kernels, all_sum(): pl.pallas_call(functools.partial(sum_kernel, sizes), out_shape=jax.ShapeD...  40.4 us
    pallas_call x1, Pallas kernels, sketch_scatter(): pl.pallas_call(functools.partial(scatter_kernel, nx), out_shape=jax.Shape...  28.1 us
    pallas_call x1, Pallas kernels, factor(): pl.pallas_call(functools.partial(factor_kernel, b), out_shape=(jax.ShapeD...  26.2 us
    unnamed x9, local copies, waits for them, and re-layouts  3.43 us

profile of v8, /device:TPU:1, one launch (start us, length us, event | category | flops | bytes accessed | tf_op | source)
XLA Modules:
  0.0 103.6 jit_solution(10330869355313570381)
XLA Ops:
  0.6 0.0 copy-start
  0.6 0.0 copy-start.1
  0.7 1.6 %copy-done.1 = bf16[2048,512]{1,0:T(8,128)(2,1)S(1)} copy-done((bf16[2048,512]{1,0:T(8,128)(2,1)S(1)}, bf16[2048,512]{1,0:T(8,128)(2,1)}, u32[]{:S(2)}) %copy-start.1) | copy-done | bytes 2097176
  2.3 0.0 copy-start.2
  2.3 0.9 copy-done.2
  3.2 28.1 %shard_map.50 = f32[512,256]{1,0:T(8,128)S(1)} custom-call(bf16[2048,512]{1,0:T(8,128)(2,1)S(1)} %copy-done.1, bf16[512,256]{1,0:T(8,128)(2,1)S(1)} %copy-done.2), custom_call_target="tpu_custom_call" | custom-call | tf_op jit(solution)/shard_map/pallas_call | solution.py:148
  31.4 1.7 %fusion.a_ref = f32[256,256]{1,0:T(8,128)} fusion(f32[512,256]{1,0:T(8,128)S(1)} %shard_map.50), kind=kOutput, calls=%fused_computation.2 | convolution fusion | flops 402653184 | bytes 786432 | tf_op jit(solution)/shard_map/dot_general | solution.py:217
  33.1 40.4 %shard_map.51.g_ref = f32[256,256]{1,0:T(8,128)} custom-call(f32[256,256]{1,0:T(8,128)} %fusion.a_ref), custom_call_target="tpu_custom_call" | custom-call | tf_op jit(solution)/shard_map/pallas_call | solution.py:88
  73.5 26.2 %shard_map.52 = (f32[256,256]{1,0:T(8,128)}, f32[256,256]{1,0:T(8,128)}) custom-call(f32[256,256]{1,0:T(8,128)} %shard_map.51.g_ref), custom_call_target="tpu_custom_call" | custom-call | tf_op jit(solution)/shard_map/pallas_call | solution.py:207
  99.7 0.0 copy-start.3
  99.7 0.0 copy-done
  99.7 1.6 %fusion.1 = f32[256,256]{1,0:T(8,128)S(1)} fusion(f32[256,256]{1,0:T(8,128)} %get-tuple-element.4, f32[256,256]{1,0:T(8,128)S(1)} %copy-done), kind=kOutput, calls=%fused_computation.3 | convolution fusion | flops 201326592 | bytes 786432 | tf_op jit(solution)/shard_map/dot_general | solution.py:226
  101.3 1.4 %convolution_multiply_fusion = f32[512,256]{1,0:T(8,128)} fusion(f32[512,256]{1,0:T(8,128)S(1)} %shard_map.50, f32[256,256]{1,0:T(8,128)S(1)} %fusion.1), kind=kOutput, calls=%fused_computation | convolution fusion | flops 402784256 | bytes 1310720 | tf_op jit(solution)/shard_map/dot_general | solution.py:232
  102.7 0.0 copy-done.3
  102.7 0.8 copy.5
  (1 shorter events, 0.0 us)
Async XLA Ops:
  0.6 99.1 %copy-start = (f32[256,256]{1,0:T(8,128)S(1)}, f32[256,256]{1,0:T(8,128)}, u32[]{:S(2)}) copy-start(f32[256,256]{1,0:T(8,128)} %param.5) | copy-start | bytes 786436
  0.6 1.6 %copy-start.1 = (bf16[2048,512]{1,0:T(8,128)(2,1)S(1)}, bf16[2048,512]{1,0:T(8,128)(2,1)}, u32[]{:S(2)}) copy-start(bf16[2048,512]{1,0:T(8,128)(2,1)} %s_ref.1) | copy-start | bytes 6291460
  2.3 0.9 copy-start.2
  99.7 3.0 %copy-start.3 = (f32[256,256]{1,0:T(8,128)S(1)}, f32[256,256]{1,0:T(8,128)}, u32[]{:S(2)}) copy-start(f32[256,256]{1,0:T(8,128)} %get-tuple-element.5) | copy-start | bytes 786436

commit v9 on v8

--- a/solution.py
+++ b/solution.py
@@ -12,23 +12,21 @@
 SPACE = ("z", "y", "c")
 
 
-def sum_kernel(sizes, a_ref, o_ref, cbuf, csum, qbuf, qsum, zbuf, full,
-               cr, cs, qr, qs, zr, zs, qgr, qgs, cgr, cgs):
+def sum_kernel(sizes, a_ref, o_ref, qbuf, qsum, zbuf, full, qr, qs, zr, zs, qgr, qgs):
     nz, ny, nc, nx = sizes
-    nq = nx * ny
+    nq = nc * nx * ny
     zi, yi, ci, xi = (lax.axis_index(a) for a in AXES)
-    qi = xi * ny + yi
+    qi = (ci * nx + xi) * ny + yi
 
     def peers(n, me):
         return [lax.rem(me + d, n) for d in range(1, n)]
 
     zdev = lambda j: (j, yi, ci, xi)
-    cdev = lambda j: (zi, yi, j, xi)
-    qdev = lambda q: (zi, lax.rem(q, ny), ci, q // ny)
+    qdev = lambda q: (zi, lax.rem(q, ny), q // (nx * ny), lax.rem(q // ny, nx))
 
     barrier = pltpu.get_barrier_semaphore()
     count = 0
-    for n, me, make in ((nz, zi, zdev), (nq, qi, qdev), (nc, ci, cdev)):
+    for n, me, make in ((nz, zi, zdev), (nq, qi, qdev)):
         for j in peers(n, me):
             pl.semaphore_signal(barrier, inc=1, device_id=make(j), device_id_type=MESH)
             count += 1
@@ -55,34 +53,26 @@
             acc = acc + buf[j]
         return acc
 
-    c1 = a_ref.shape[0] // nc
-    c2 = c1 // nq
-
-    cbuf[ci] = a_ref[pl.ds(ci * c1, c1)]
-    exchange(nc, ci, cdev, lambda j: a_ref.at[pl.ds(j * c1, c1)], lambda j: cbuf.at[j], cr, cs)
-    csum[...] = ordered_sum(cbuf, nc)
-
-    qbuf[qi] = csum[pl.ds(qi * c2, c2)]
-    exchange(nq, qi, qdev, lambda j: csum.at[pl.ds(j * c2, c2)], lambda j: qbuf.at[j], qr, qs)
+    c1 = a_ref.shape[0] // nq
+
+    qbuf[qi] = a_ref[pl.ds(qi * c1, c1)]
+    exchange(nq, qi, qdev, lambda j: a_ref.at[pl.ds(j * c1, c1)], lambda j: qbuf.at[j], qr, qs)
     qsum[...] = ordered_sum(qbuf, nq)
 
     zbuf[zi] = qsum[...]
     exchange(nz, zi, zdev, lambda j: qsum, lambda j: zbuf.at[j], zr, zs)
-    own = ci * c1 + qi * c2
-    full[pl.ds(own, c2)] = ordered_sum(zbuf, nz)
-
-    exchange(nq, qi, qdev, lambda j: full.at[pl.ds(own, c2)],
-             lambda j: full.at[pl.ds(ci * c1 + j * c2, c2)], qgr, qgs)
-    exchange(nc, ci, cdev, lambda j: full.at[pl.ds(ci * c1, c1)],
-             lambda j: full.at[pl.ds(j * c1, c1)], cgr, cgs)
+    own = qi * c1
+    full[pl.ds(own, c1)] = ordered_sum(zbuf, nz)
+
+    exchange(nq, qi, qdev, lambda j: full.at[pl.ds(own, c1)],
+             lambda j: full.at[pl.ds(j * c1, c1)], qgr, qgs)
     o_ref[...] = full[...]
 
 
 def all_sum(gram, sizes):
     nz, ny, nc, nx = sizes
-    nq = nx * ny
-    c1 = gram.shape[0] // nc
-    c2 = c1 // nq
+    nq = nc * nx * ny
+    c1 = gram.shape[0] // nq
     t = gram.shape[1:]
     dma = pltpu.SemaphoreType.DMA
     return pl.pallas_call(
@@ -91,15 +81,11 @@
         in_specs=[pl.BlockSpec(memory_space=pltpu.VMEM)],
         out_specs=pl.BlockSpec(memory_space=pltpu.VMEM),
         scratch_shapes=[
-            pltpu.VMEM((nc, c1) + t, jnp.float32),
+            pltpu.VMEM((nq, c1) + t, jnp.float32),
             pltpu.VMEM((c1,) + t, jnp.float32),
-            pltpu.VMEM((nq, c2) + t, jnp.float32),
-            pltpu.VMEM((c2,) + t, jnp.float32),
-            pltpu.VMEM((nz, c2) + t, jnp.float32),
+            pltpu.VMEM((nz, c1) + t, jnp.float32),
             pltpu.VMEM(gram.shape, jnp.float32),
-            dma((nc,)), dma((nc,)), dma((nq,)), dma((nq,)),
-            dma((nz,)), dma((nz,)), dma((nq,)), dma((nq,)),
-            dma((nc,)), dma((nc,)),
+            dma((nq,)), dma((nq,)), dma((nz,)), dma((nz,)), dma((nq,)), dma((nq,)),
         ],
         compiler_params=pltpu.CompilerParams(collective_id=0, has_side_effects=True),
     )(gram)

time: 104 us -> 103 us (level)
  no operation moved by 1% of the time
where the time goes in v9:
time: 103 us
  Pallas kernels  94.3 us (92%)
  matrix products  4.69 us (5%)
  local copies, waits for them, and re-layouts  3.43 us (3%)
    pallas_call x1, Pallas kernels, all_sum(): pl.pallas_call(functools.partial(sum_kernel, sizes), out_shape=jax.ShapeD...  39.9 us
    pallas_call x1, Pallas kernels, sketch_scatter(): pl.pallas_call(functools.partial(scatter_kernel, nx), out_shape=jax.Shape...  28.1 us
    pallas_call x1, Pallas kernels, factor(): pl.pallas_call(functools.partial(factor_kernel, b), out_shape=(jax.ShapeD...  26.2 us
    unnamed x9, local copies, waits for them, and re-layouts  3.43 us

profile of v9, /device:TPU:1, one launch (start us, length us, event | category | flops | bytes accessed | tf_op | source)
XLA Modules:
  0.0 103.1 jit_solution(342362497439736074)
XLA Ops:
  0.6 0.0 copy-start
  0.6 0.0 copy-start.1
  0.7 1.6 %copy-done.1 = bf16[2048,512]{1,0:T(8,128)(2,1)S(1)} copy-done((bf16[2048,512]{1,0:T(8,128)(2,1)S(1)}, bf16[2048,512]{1,0:T(8,128)(2,1)}, u32[]{:S(2)}) %copy-start.1) | copy-done | bytes 2097176
  2.3 0.0 copy-start.2
  2.3 0.9 copy-done.2
  3.2 28.1 %shard_map.50 = f32[512,256]{1,0:T(8,128)S(1)} custom-call(bf16[2048,512]{1,0:T(8,128)(2,1)S(1)} %copy-done.1, bf16[512,256]{1,0:T(8,128)(2,1)S(1)} %copy-done.2), custom_call_target="tpu_custom_call" | custom-call | tf_op jit(solution)/shard_map/pallas_call | solution.py:134
  31.4 1.7 %fusion.a_ref = f32[256,256]{1,0:T(8,128)} fusion(f32[512,256]{1,0:T(8,128)S(1)} %shard_map.50), kind=kOutput, calls=%fused_computation.2 | convolution fusion | flops 402653184 | bytes 786432 | tf_op jit(solution)/shard_map/dot_general | solution.py:203
  33.1 39.9 %shard_map.51.g_ref = f32[256,256]{1,0:T(8,128)} custom-call(f32[256,256]{1,0:T(8,128)} %fusion.a_ref), custom_call_target="tpu_custom_call" | custom-call | tf_op jit(solution)/shard_map/pallas_call | solution.py:78
  73.0 26.2 %shard_map.52 = (f32[256,256]{1,0:T(8,128)}, f32[256,256]{1,0:T(8,128)}) custom-call(f32[256,256]{1,0:T(8,128)} %shard_map.51.g_ref), custom_call_target="tpu_custom_call" | custom-call | tf_op jit(solution)/shard_map/pallas_call | solution.py:193
  99.3 0.0 copy-start.3
  99.3 0.0 copy-done
  99.3 1.6 %fusion.1 = f32[256,256]{1,0:T(8,128)S(1)} fusion(f32[256,256]{1,0:T(8,128)} %get-tuple-element.4, f32[256,256]{1,0:T(8,128)S(1)} %copy-done), kind=kOutput, calls=%fused_computation.3 | convolution fusion | flops 201326592 | bytes 786432 | tf_op jit(solution)/shard_map/dot_general | solution.py:212
  100.8 1.4 %convolution_multiply_fusion = f32[512,256]{1,0:T(8,128)} fusion(f32[512,256]{1,0:T(8,128)S(1)} %shard_map.50, f32[256,256]{1,0:T(8,128)S(1)} %fusion.1), kind=kOutput, calls=%fused_computation | convolution fusion | flops 402784256 | bytes 1310720 | tf_op jit(solution)/shard_map/dot_general | solution.py:218
  102.2 0.0 copy-done.3
  102.2 0.8 copy.5
  (1 shorter events, 0.0 us)
Async XLA Ops:
  0.6 98.6 %copy-start = (f32[256,256]{1,0:T(8,128)S(1)}, f32[256,256]{1,0:T(8,128)}, u32[]{:S(2)}) copy-start(f32[256,256]{1,0:T(8,128)} %param.5) | copy-start | bytes 786436
  0.6 1.6 %copy-start.1 = (bf16[2048,512]{1,0:T(8,128)(2,1)S(1)}, bf16[2048,512]{1,0:T(8,128)(2,1)}, u32[]{:S(2)}) copy-start(bf16[2048,512]{1,0:T(8,128)(2,1)} %s_ref.1) | copy-start | bytes 6291460
  2.3 0.9 copy-start.2
  99.3 3.0 %copy-start.3 = (f32[256,256]{1,0:T(8,128)S(1)}, f32[256,256]{1,0:T(8,128)}, u32[]{:S(2)}) copy-start(f32[256,256]{1,0:T(8,128)} %get-tuple-element.5) | copy-start | bytes 786436

commit v10 on v9

--- a/solution.py
+++ b/solution.py
@@ -1,6 +1,7 @@
 import functools
 
 import jax
+import numpy as np
 import jax.numpy as jnp
 from jax import lax
 from jax.experimental import pallas as pl
@@ -146,7 +147,7 @@
     )(snapshots, sketch)
 
 
-def factor_kernel(b, g_ref, l_ref, w_ref):
+def factor_kernel(b, scale, g_ref, q_ref, r_ref, basis_ref, tri_ref, l_ref, w_ref):
     n = g_ref.shape[0]
     hi = lax.Precision.HIGHEST
     l_ref[...] = jnp.zeros_like(l_ref)
@@ -186,16 +187,23 @@
         return carry
 
     lax.fori_loop(0, n // b, panel, 0)
-
-
-def factor(gram, b=128):
+    rotated = lax.dot_general(w_ref[...], r_ref[...], (((0,), (0,)), ((), ())), precision=hi,
+                              preferred_element_type=jnp.float32)
+    basis_ref[...] = scale * jnp.dot(q_ref[...], rotated, precision=hi,
+                                     preferred_element_type=jnp.float32)
+    tri_ref[...] = l_ref[...].T / scale
+
+
+def factor(gram, sketched, rotation, scale, b=128):
     n = gram.shape[0]
     return pl.pallas_call(
-        functools.partial(factor_kernel, b),
-        out_shape=(jax.ShapeDtypeStruct((n, n), jnp.float32),) * 2,
-        in_specs=[pl.BlockSpec(memory_space=pltpu.VMEM)],
+        functools.partial(factor_kernel, b, scale),
+        out_shape=(jax.ShapeDtypeStruct(sketched.shape, jnp.float32),
+                   jax.ShapeDtypeStruct((n, n), jnp.float32)),
+        in_specs=[pl.BlockSpec(memory_space=pltpu.VMEM)] * 3,
         out_specs=(pl.BlockSpec(memory_space=pltpu.VMEM),) * 2,
-    )(gram)
+        scratch_shapes=[pltpu.VMEM((n, n), jnp.float32)] * 2,
+    )(gram, sketched, rotation)
 
 
 def shards(sizes, snapshots, sketch, rotation):
@@ -208,17 +216,9 @@
         preferred_element_type=jnp.float32,
     )
     gram = all_sum(gram, sizes)
-    lower, inverse = factor(gram)
-    rotated = lax.dot_general(
-        inverse, rotation, (((0,), (0,)), ((), ())),
-        precision=lax.Precision.HIGHEST, preferred_element_type=jnp.float32,
-    )
     cell_count = sketched.shape[0] * sizes[0] * sizes[1] * sizes[2] * sizes[3]
-    scale = jnp.sqrt(jnp.float32(cell_count))
-    basis = scale * jnp.dot(
-        sketched, rotated, precision=lax.Precision.HIGHEST, preferred_element_type=jnp.float32
-    )
-    triangle = lower.T / scale
+    scale = float(np.sqrt(np.float32(cell_count)))
+    basis, triangle = factor(gram, sketched, rotation, scale)
     return (basis, triangle)
 
 

time: 103 us -> 101 us (0.981)
  matrix products: 4.69 us -> 1.73 us
  Pallas kernels: 94.3 us -> 96 us
    dot_general x2 -> x0, matrix products: 2.96 us -> none  [the longest x1 1.58 us: shards(): lax.dot_general(inverse, rotation, (((0,), (0,)), ((), ())), precision=la...]
    pallas_call x1, Pallas kernels: 26.2 us -> 27.9 us  [factor(): pl.pallas_call(functools.partial(factor_kernel, b, scale), out_shape=(jax...]
    unnamed x9 -> x6, local copies, waits for them, and re-layouts: 3.43 us -> 2.54 us
where the time goes in v10:
time: 101 us
  Pallas kernels  96 us (95%)
  local copies, waits for them, and re-layouts  2.54 us (3%)
  matrix products  1.73 us (2%)
    pallas_call x1, Pallas kernels, all_sum(): pl.pallas_call(functools.partial(sum_kernel, sizes), out_shape=jax.ShapeD...  39.9 us
    pallas_call x1, Pallas kernels, sketch_scatter(): pl.pallas_call(functools.partial(scatter_kernel, nx), out_shape=jax.Shape...  28.1 us
    pallas_call x1, Pallas kernels, factor(): pl.pallas_call(functools.partial(factor_kernel, b, scale), out_shape=(jax...  27.9 us
    unnamed x6, local copies, waits for them, and re-layouts  2.54 us

profile of v10, /device:TPU:1, one launch (start us, length us, event | category | flops | bytes accessed | tf_op | source)
XLA Modules:
  0.0 100.9 jit_solution(7049387265242211038)
XLA Ops:
  0.6 0.0 copy-start.1
  0.6 1.6 %copy-done.1 = bf16[2048,512]{1,0:T(8,128)(2,1)S(1)} copy-done((bf16[2048,512]{1,0:T(8,128)(2,1)S(1)}, bf16[2048,512]{1,0:T(8,128)(2,1)}, u32[]{:S(2)}) %copy-start.1) | copy-done | bytes 2097176
  2.2 0.0 copy-start.2
  2.2 0.9 copy-done.2
  3.2 28.1 %shard_map.50.q_ref = f32[512,256]{1,0:T(8,128)S(1)} custom-call(bf16[2048,512]{1,0:T(8,128)(2,1)S(1)} %copy-done.1, bf16[512,256]{1,0:T(8,128)(2,1)S(1)} %copy-done.2), custom_call_target="tpu_custom_call" | custom-call | tf_op jit(solution)/shard_map/pallas_call | solution.py:135
  31.3 0.0 copy-start
  31.3 1.7 %fusion.a_ref = f32[256,256]{1,0:T(8,128)} fusion(f32[512,256]{1,0:T(8,128)S(1)} %shard_map.50.q_ref), kind=kOutput, calls=%fused_computation | convolution fusion | flops 402653184 | bytes 786432 | tf_op jit(solution)/shard_map/dot_general | solution.py:211
  33.0 39.9 %shard_map.51.g_ref = f32[256,256]{1,0:T(8,128)} custom-call(f32[256,256]{1,0:T(8,128)} %fusion.a_ref), custom_call_target="tpu_custom_call" | custom-call | tf_op jit(solution)/shard_map/pallas_call | solution.py:79
  73.0 0.0 copy-done
  73.0 27.9 %shard_map.52 = (f32[512,256]{1,0:T(8,128)}, f32[256,256]{1,0:T(8,128)}) custom-call(f32[256,256]{1,0:T(8,128)} %shard_map.51.g_ref, f32[512,256]{1,0:T(8,128)} %copy-done, f32[256,256]{1,0:T(8,128)} %r_ref.1), custom_call_target="tpu_custom_call" | custom-call | tf_op jit(solution)/shard_map/pallas_call | solution.py:199
Async XLA Ops:
  0.6 1.6 %copy-start.1 = (bf16[2048,512]{1,0:T(8,128)(2,1)S(1)}, bf16[2048,512]{1,0:T(8,128)(2,1)}, u32[]{:S(2)}) copy-start(bf16[2048,512]{1,0:T(8,128)(2,1)} %s_ref.1) | copy-start | bytes 6291460
  2.2 0.9 copy-start.2
  31.3 41.7 %copy-start = (f32[512,256]{1,0:T(8,128)}, f32[512,256]{1,0:T(8,128)S(1)}, u32[]{:S(2)}) copy-start(f32[512,256]{1,0:T(8,128)S(1)} %shard_map.50.q_ref) | copy-start | bytes 1572868

commit v11 on v10

--- a/solution.py
+++ b/solution.py
@@ -13,7 +13,7 @@
 SPACE = ("z", "y", "c")
 
 
-def sum_kernel(sizes, a_ref, o_ref, qbuf, qsum, zbuf, full, qr, qs, zr, zs, qgr, qgs):
+def sum_kernel(sizes, q_ref, o_ref, a_ref, qbuf, qsum, zbuf, full, qr, qs, zr, zs, qgr, qgs):
     nz, ny, nc, nx = sizes
     nq = nc * nx * ny
     zi, yi, ci, xi = (lax.axis_index(a) for a in AXES)
@@ -24,6 +24,10 @@
 
     zdev = lambda j: (j, yi, ci, xi)
     qdev = lambda q: (zi, lax.rem(q, ny), q // (nx * ny), lax.rem(q // ny, nx))
+
+    a_ref[...] = lax.dot_general(q_ref[...], q_ref[...], (((0,), (0,)), ((), ())),
+                                 precision=lax.Precision.HIGHEST,
+                                 preferred_element_type=jnp.float32)
 
     barrier = pltpu.get_barrier_semaphore()
     count = 0
@@ -70,11 +74,13 @@
     o_ref[...] = full[...]
 
 
-def all_sum(gram, sizes):
+def all_sum(sketched, sizes):
     nz, ny, nc, nx = sizes
     nq = nc * nx * ny
-    c1 = gram.shape[0] // nq
-    t = gram.shape[1:]
+    k = sketched.shape[1]
+    gram = jax.ShapeDtypeStruct((k, k), jnp.float32)
+    c1 = k // nq
+    t = (k,)
     dma = pltpu.SemaphoreType.DMA
     return pl.pallas_call(
         functools.partial(sum_kernel, sizes),
@@ -82,6 +88,7 @@
         in_specs=[pl.BlockSpec(memory_space=pltpu.VMEM)],
         out_specs=pl.BlockSpec(memory_space=pltpu.VMEM),
         scratch_shapes=[
+            pltpu.VMEM(gram.shape, jnp.float32),
             pltpu.VMEM((nq, c1) + t, jnp.float32),
             pltpu.VMEM((c1,) + t, jnp.float32),
             pltpu.VMEM((nz, c1) + t, jnp.float32),
@@ -89,12 +96,23 @@
             dma((nq,)), dma((nq,)), dma((nz,)), dma((nz,)), dma((nq,)), dma((nq,)),
         ],
         compiler_params=pltpu.CompilerParams(collective_id=0, has_side_effects=True),
-    )(gram)
-
-
-def scatter_kernel(nx, s_ref, k_ref, o_ref, part, rbuf, rs, ss):
+    )(sketched)
+
+
+def scatter_kernel(nx, s_hbm, k_hbm, o_ref, s_ref, k_ref, part, rbuf, rs, ss, ls):
     xi = lax.axis_index("x")
     rows = o_ref.shape[0]
+    fetch = [pltpu.make_async_copy(k_hbm, k_ref, ls.at[nx])]
+    for j in range(nx):
+        fetch.append(pltpu.make_async_copy(s_hbm.at[pl.ds(j * rows, rows)],
+                                           s_ref.at[pl.ds(j * rows, rows)], ls.at[j]))
+    for cp in fetch:
+        cp.start()
+    fetch[0].wait()
+
+    def fetched(j):
+        pltpu.make_async_copy(s_hbm.at[pl.ds(j * rows, rows)],
+                              s_ref.at[pl.ds(j * rows, rows)], ls.at[j]).wait()
 
     barrier = pltpu.get_barrier_semaphore()
     for d in range(1, nx):
@@ -105,6 +123,7 @@
     copies = []
     for d in range(1, nx):
         j = lax.rem(xi + d, nx)
+        fetched(j)
         block = s_ref[pl.ds(pl.multiple_of(j * rows, rows), rows), :]
         part[j] = jnp.dot(block, k_ref[...], preferred_element_type=jnp.float32)
         cp = pltpu.make_async_remote_copy(
@@ -112,6 +131,7 @@
             recv_sem=rs.at[xi], device_id={"x": j}, device_id_type=MESH)
         cp.start()
         copies.append(cp)
+    fetched(xi)
     block = s_ref[pl.ds(pl.multiple_of(xi * rows, rows), rows), :]
     rbuf[xi] = jnp.dot(block, k_ref[...], preferred_element_type=jnp.float32)
     for d in range(1, nx):
@@ -135,15 +155,16 @@
     return pl.pallas_call(
         functools.partial(scatter_kernel, nx),
         out_shape=jax.ShapeDtypeStruct((rows, cols), jnp.float32),
-        in_specs=[pl.BlockSpec(memory_space=pltpu.VMEM)] * 2,
+        in_specs=[pl.BlockSpec(memory_space=pl.ANY)] * 2,
         out_specs=pl.BlockSpec(memory_space=pltpu.VMEM),
         scratch_shapes=[
+            pltpu.VMEM(snapshots.shape, snapshots.dtype),
+            pltpu.VMEM(sketch.shape, sketch.dtype),
             pltpu.VMEM((nx, rows, cols), jnp.float32),
             pltpu.VMEM((nx, rows, cols), jnp.float32),
-            dma((nx,)), dma((nx,)),
+            dma((nx,)), dma((nx,)), dma((nx + 1,)),
         ],
-        compiler_params=pltpu.CompilerParams(collective_id=1, has_side_effects=True,
-                                             vmem_limit_bytes=48 * 1024 * 1024),
+        compiler_params=pltpu.CompilerParams(collective_id=1, has_side_effects=True),
     )(snapshots, sketch)
 
 
@@ -208,14 +229,7 @@
 
 def shards(sizes, snapshots, sketch, rotation):
     sketched = sketch_scatter(snapshots, sketch, sizes[3])
-    gram = lax.dot_general(
-        sketched,
-        sketched,
-        (((0,), (0,)), ((), ())),
-        precision=lax.Precision.HIGHEST,
-        preferred_element_type=jnp.float32,
-    )
-    gram = all_sum(gram, sizes)
+    gram = all_sum(sketched, sizes)
     cell_count = sketched.shape[0] * sizes[0] * sizes[1] * sizes[2] * sizes[3]
     scale = float(np.sqrt(np.float32(cell_count)))
     basis, triangle = factor(gram, sketched, rotation, scale)

time: 101 us -> 100 us (0.990)
  Pallas kernels: 96 us -> 99.3 us
  local copies, waits for them, and re-layouts: 2.54 us -> 0 us
  matrix products: 1.73 us -> 0 us
    unnamed x6 -> x0, local copies, waits for them, and re-layouts: 2.54 us -> none
    pallas_call x1, Pallas kernels: 28.1 us -> 29.9 us  [sketch_scatter(): pl.pallas_call(functools.partial(scatter_kernel, nx), out_shape=jax.Shape...]
    dot_general x1 -> x0, matrix products: 1.73 us -> none  [shards(): lax.dot_general(sketched, sketched, (((0,), (0,)), ((), ())), precision=l...]
    pallas_call x1, Pallas kernels: 39.9 us -> 41.6 us  [all_sum(): pl.pallas_call(functools.partial(sum_kernel, sizes), out_shape=jax.ShapeD...]
where the time goes in v11:
time: 100 us
  Pallas kernels  99.3 us (99%)
    pallas_call x1, Pallas kernels, all_sum(): pl.pallas_call(functools.partial(sum_kernel, sizes), out_shape=jax.ShapeD...  41.6 us
    pallas_call x1, Pallas kernels, sketch_scatter(): pl.pallas_call(functools.partial(scatter_kernel, nx), out_shape=jax.Shape...  29.9 us
    pallas_call x1, Pallas kernels, factor(): pl.pallas_call(functools.partial(factor_kernel, b, scale), out_shape=(jax...  27.9 us

profile of v11, /device:TPU:1, one launch (start us, length us, event | category | flops | bytes accessed | tf_op | source)
XLA Modules:
  0.0 100.0 jit_solution(13888790969712213248)
XLA Ops:
  0.6 29.9 %shard_map.50.q_ref = f32[512,256]{1,0:T(8,128)} custom-call(bf16[2048,512]{1,0:T(8,128)(2,1)} %s_hbm.1, bf16[512,256]{1,0:T(8,128)(2,1)} %k_hbm.1), custom_call_target="tpu_custom_call" | custom-call | tf_op jit(solution)/shard_map/pallas_call | solution.py:155
  30.5 41.6 %shard_map.51.g_ref = f32[256,256]{1,0:T(8,128)} custom-call(f32[512,256]{1,0:T(8,128)} %shard_map.50.q_ref), custom_call_target="tpu_custom_call" | custom-call | tf_op jit(solution)/shard_map/pallas_call | solution.py:85
  72.1 27.9 %shard_map.52 = (f32[512,256]{1,0:T(8,128)}, f32[256,256]{1,0:T(8,128)}) custom-call(f32[256,256]{1,0:T(8,128)} %shard_map.51.g_ref, f32[512,256]{1,0:T(8,128)} %shard_map.50.q_ref, f32[256,256]{1,0:T(8,128)} %r_ref.1), custom_call_target="tpu_custom_call" | custom-call | tf_op jit(solution)/shard_map/pallas_call | solution.py:220

commit v12 on v11

--- a/solution.py
+++ b/solution.py
@@ -99,9 +99,11 @@
     )(sketched)
 
 
-def scatter_kernel(nx, s_hbm, k_hbm, o_ref, s_ref, k_ref, part, rbuf, rs, ss, ls):
+def scatter_kernel(nx, s_hbm, k_hbm, o_ref, s_ref, k_ref, part, rbuf, relay, rs, rh, rl, ss, ls):
     xi = lax.axis_index("x")
     rows = o_ref.shape[0]
+    half = rows // 2
+    right, left, opp = lax.rem(xi + 1, nx), lax.rem(xi + nx - 1, nx), lax.rem(xi + 2, nx)
     fetch = [pltpu.make_async_copy(k_hbm, k_ref, ls.at[nx])]
     for j in range(nx):
         fetch.append(pltpu.make_async_copy(s_hbm.at[pl.ds(j * rows, rows)],
@@ -110,40 +112,50 @@
         cp.start()
     fetch[0].wait()
 
-    def fetched(j):
+    def compute(j):
         pltpu.make_async_copy(s_hbm.at[pl.ds(j * rows, rows)],
                               s_ref.at[pl.ds(j * rows, rows)], ls.at[j]).wait()
+        block = s_ref[pl.ds(pl.multiple_of(j * rows, rows), rows), :]
+        return jnp.dot(block, k_ref[...], preferred_element_type=jnp.float32)
+
+    def send(src, dst, sem_send, sem_recv, dev):
+        return pltpu.make_async_remote_copy(
+            src_ref=src, dst_ref=dst, send_sem=sem_send, recv_sem=sem_recv,
+            device_id={"x": dev}, device_id_type=MESH)
 
     barrier = pltpu.get_barrier_semaphore()
-    for d in range(1, nx):
-        pl.semaphore_signal(barrier, inc=1, device_id={"x": lax.rem(xi + d, nx)},
-                            device_id_type=MESH)
-    pl.semaphore_wait(barrier, nx - 1)
-
-    copies = []
-    for d in range(1, nx):
-        j = lax.rem(xi + d, nx)
-        fetched(j)
-        block = s_ref[pl.ds(pl.multiple_of(j * rows, rows), rows), :]
-        part[j] = jnp.dot(block, k_ref[...], preferred_element_type=jnp.float32)
-        cp = pltpu.make_async_remote_copy(
-            src_ref=part.at[j], dst_ref=rbuf.at[xi], send_sem=ss.at[j],
-            recv_sem=rs.at[xi], device_id={"x": j}, device_id_type=MESH)
+    for dev in (left, right):
+        pl.semaphore_signal(barrier, inc=1, device_id={"x": dev}, device_id_type=MESH)
+    pl.semaphore_wait(barrier, 2)
+
+    part[0] = compute(opp)
+    lo, hi = pl.ds(0, half), pl.ds(half, half)
+    out = [send(part.at[0, lo], relay.at[0], ss.at[0], rl.at[0], right),
+           send(part.at[0, hi], relay.at[1], ss.at[1], rl.at[1], left)]
+    part[1] = compute(right)
+    out.append(send(part.at[1], rbuf.at[xi], ss.at[2], rs.at[0], right))
+    part[2] = compute(left)
+    out.append(send(part.at[2], rbuf.at[xi], ss.at[3], rs.at[1], left))
+    for cp in out[:2]:
         cp.start()
-        copies.append(cp)
-    fetched(xi)
-    block = s_ref[pl.ds(pl.multiple_of(xi * rows, rows), rows), :]
-    rbuf[xi] = jnp.dot(block, k_ref[...], preferred_element_type=jnp.float32)
-    for d in range(1, nx):
-        j = lax.rem(xi + d, nx)
-        pltpu.make_async_remote_copy(
-            src_ref=part.at[j], dst_ref=rbuf.at[j], send_sem=ss.at[j],
-            recv_sem=rs.at[j], device_id={"x": j}, device_id_type=MESH).wait_recv()
+    for cp in out[2:]:
+        cp.start()
+    send(part.at[0, lo], relay.at[0], ss.at[0], rl.at[0], left).wait_recv()
+    fwd = [send(relay.at[0], rbuf.at[left, lo], ss.at[4], rh.at[0], right)]
+    fwd[0].start()
+    send(part.at[0, hi], relay.at[1], ss.at[1], rl.at[1], right).wait_recv()
+    fwd.append(send(relay.at[1], rbuf.at[right, hi], ss.at[5], rh.at[1], left))
+    fwd[1].start()
+    rbuf[xi] = compute(xi)
+    send(part.at[1], rbuf.at[left], ss.at[2], rs.at[0], left).wait_recv()
+    send(part.at[2], rbuf.at[right], ss.at[3], rs.at[1], right).wait_recv()
+    send(relay.at[0], rbuf.at[opp, lo], ss.at[4], rh.at[0], left).wait_recv()
+    send(relay.at[1], rbuf.at[opp, hi], ss.at[5], rh.at[1], right).wait_recv()
     acc = rbuf[0]
     for j in range(1, nx):
         acc = acc + rbuf[j]
     o_ref[...] = acc
-    for cp in copies:
+    for cp in out + fwd:
         cp.wait_send()
 
 
@@ -160,9 +172,10 @@
         scratch_shapes=[
             pltpu.VMEM(snapshots.shape, snapshots.dtype),
             pltpu.VMEM(sketch.shape, sketch.dtype),
+            pltpu.VMEM((3, rows, cols), jnp.float32),
             pltpu.VMEM((nx, rows, cols), jnp.float32),
-            pltpu.VMEM((nx, rows, cols), jnp.float32),
-            dma((nx,)), dma((nx,)), dma((nx + 1,)),
+            pltpu.VMEM((2, rows // 2, cols), jnp.float32),
+            dma((2,)), dma((2,)), dma((2,)), dma((6,)), dma((nx + 1,)),
         ],
         compiler_params=pltpu.CompilerParams(collective_id=1, has_side_effects=True),
     )(snapshots, sketch)

time: 100 us -> 100 us (level)
    pallas_call x1, Pallas kernels: 41.6 us -> 45.8 us  [all_sum(): pl.pallas_call(functools.partial(sum_kernel, sizes), out_shape=jax.ShapeD...]
    pallas_call x1, Pallas kernels: 29.9 us -> 25.8 us  [sketch_scatter(): pl.pallas_call(functools.partial(scatter_kernel, nx), out_shape=jax.Shape...]
where the time goes in v12:
time: 100 us
  Pallas kernels  99.5 us (100%)
    pallas_call x1, Pallas kernels, all_sum(): pl.pallas_call(functools.partial(sum_kernel, sizes), out_shape=jax.ShapeD...  45.8 us
    pallas_call x1, Pallas kernels, factor(): pl.pallas_call(functools.partial(factor_kernel, b, scale), out_shape=(jax...  27.9 us
    pallas_call x1, Pallas kernels, sketch_scatter(): pl.pallas_call(functools.partial(scatter_kernel, nx), out_shape=jax.Shape...  25.8 us

profile of v12, /device:TPU:1, one launch (start us, length us, event | category | flops | bytes accessed | tf_op | source)
XLA Modules:
  0.0 100.2 jit_solution(13185543390396306062)
XLA Ops:
  0.6 25.8 %shard_map.50.q_ref = f32[512,256]{1,0:T(8,128)} custom-call(bf16[2048,512]{1,0:T(8,128)(2,1)} %s_hbm.1, bf16[512,256]{1,0:T(8,128)(2,1)} %k_hbm.1), custom_call_target="tpu_custom_call" | custom-call | tf_op jit(solution)/shard_map/pallas_call | solution.py:167
  26.5 45.8 %shard_map.51.g_ref = f32[256,256]{1,0:T(8,128)} custom-call(f32[512,256]{1,0:T(8,128)} %shard_map.50.q_ref), custom_call_target="tpu_custom_call" | custom-call | tf_op jit(solution)/shard_map/pallas_call | solution.py:85
  72.2 27.9 %shard_map.52 = (f32[512,256]{1,0:T(8,128)}, f32[256,256]{1,0:T(8,128)}) custom-call(f32[256,256]{1,0:T(8,128)} %shard_map.51.g_ref, f32[512,256]{1,0:T(8,128)} %shard_map.50.q_ref, f32[256,256]{1,0:T(8,128)} %r_ref.1), custom_call_target="tpu_custom_call" | custom-call | tf_op jit(solution)/shard_map/pallas_call | solution.py:233

commit v13 on v10

v13 whole, which is shorter than its diff:
```python
import functools

import jax
import numpy as np
import jax.numpy as jnp
from jax import lax
from jax.experimental import pallas as pl
from jax.experimental.pallas import tpu as pltpu
from jax.sharding import Mesh, PartitionSpec as P

MESH = pl.DeviceIdType.MESH
AXES = ("z", "y", "c", "x")
SPACE = ("z", "y", "c")


def fused_kernel(sizes, s_hbm, k_hbm, q_out, g_out, s_ref, k_ref, part, rbuf, a_ref, qbuf,
                 qsum, zbuf, full, rs, ss, ls, qr, qs, zr, zs, qgr, qgs):
    nz, ny, nc, nx = sizes
    nq = nc * nx * ny
    zi, yi, ci, xi = (lax.axis_index(a) for a in AXES)
    qi = (ci * nx + xi) * ny + yi
    rows = q_out.shape[0]

    def peers(n, me):
        return [lax.rem(me + d, n) for d in range(1, n)]

    zdev = lambda j: (j, yi, ci, xi)
    xdev = lambda j: (zi, yi, ci, j)
    qdev = lambda q: (zi, lax.rem(q, ny), q // (nx * ny), lax.rem(q // ny, nx))

    fetch = [pltpu.make_async_copy(k_hbm, k_ref, ls.at[nx])]
    for j in range(nx):
        fetch.append(pltpu.make_async_copy(s_hbm.at[pl.ds(j * rows, rows)],
                                           s_ref.at[pl.ds(j * rows, rows)], ls.at[j]))
    for cp in fetch:
        cp.start()

    barrier = pltpu.get_barrier_semaphore()
    count = 0
    for n, me, make in ((nz, zi, zdev), (nq, qi, qdev)):
        for j in peers(n, me):
            pl.semaphore_signal(barrier, inc=1, device_id=make(j), device_id_type=MESH)
            count += 1
    fetch[0].wait()

    def fetched(j):
        pltpu.make_async_copy(s_hbm.at[pl.ds(j * rows, rows)],
                              s_ref.at[pl.ds(j * rows, rows)], ls.at[j]).wait()

    pl.semaphore_wait(barrier, count)

    copies = []
    for d in range(1, nx):
        j = lax.rem(xi + d, nx)
        fetched(j)
        block = s_ref[pl.ds(pl.multiple_of(j * rows, rows), rows), :]
        part[j] = jnp.dot(block, k_ref[...], preferred_element_type=jnp.float32)
        cp = pltpu.make_async_remote_copy(
            src_ref=part.at[j], dst_ref=rbuf.at[xi], send_sem=ss.at[j],
            recv_sem=rs.at[xi], device_id=xdev(j), device_id_type=MESH)
        cp.start()
        copies.append(cp)
    fetched(xi)
    block = s_ref[pl.ds(pl.multiple_of(xi * rows, rows), rows), :]
    rbuf[xi] = jnp.dot(block, k_ref[...], preferred_element_type=jnp.float32)
    for d in range(1, nx):
        j = lax.rem(xi + d, nx)
        pltpu.make_async_remote_copy(
            src_ref=part.at[j], dst_ref=rbuf.at[j], send_sem=ss.at[j],
            recv_sem=rs.at[j], device_id=xdev(j), device_id_type=MESH).wait_recv()
    acc = rbuf[0]
    for j in range(1, nx):
        acc = acc + rbuf[j]
    q_out[...] = acc
    for cp in copies:
        cp.wait_send()

    a_ref[...] = lax.dot_general(acc, acc, (((0,), (0,)), ((), ())),
                                 precision=lax.Precision.HIGHEST,
                                 preferred_element_type=jnp.float32)

    def exchange(n, me, make, src_of, dst_of, rsem, ssem):
        sent = []
        for j in peers(n, me):
            cp = pltpu.make_async_remote_copy(
                src_ref=src_of(j), dst_ref=dst_of(me), send_sem=ssem.at[j],
                recv_sem=rsem.at[me], device_id=make(j), device_id_type=MESH)
            cp.start()
            sent.append(cp)
        for j in peers(n, me):
            pltpu.make_async_remote_copy(
                src_ref=src_of(j), dst_ref=dst_of(j), send_sem=ssem.at[j],
                recv_sem=rsem.at[j], device_id=make(j), device_id_type=MESH).wait_recv()
        for cp in sent:
            cp.wait_send()

    def ordered_sum(buf, n):
        total = buf[0]
        for j in range(1, n):
            total = total + buf[j]
        return total

    c1 = a_ref.shape[0] // nq

    qbuf[qi] = a_ref[pl.ds(qi * c1, c1)]
    exchange(nq, qi, qdev, lambda j: a_ref.at[pl.ds(j * c1, c1)], lambda j: qbuf.at[j], qr, qs)
    qsum[...] = ordered_sum(qbuf, nq)

    zbuf[zi] = qsum[...]
    exchange(nz, zi, zdev, lambda j: qsum, lambda j: zbuf.at[j], zr, zs)
    own = qi * c1
    full[pl.ds(own, c1)] = ordered_sum(zbuf, nz)

    exchange(nq, qi, qdev, lambda j: full.at[pl.ds(own, c1)],
             lambda j: full.at[pl.ds(j * c1, c1)], qgr, qgs)
    g_out[...] = full[...]


def sketch_and_gram(snapshots, sketch, sizes):
    nz, ny, nc, nx = sizes
    nq = nc * nx * ny
    rows = snapshots.shape[0] // nx
    k = sketch.shape[1]
    c1 = k // nq
    dma = pltpu.SemaphoreType.DMA
    return pl.pallas_call(
        functools.partial(fused_kernel, sizes),
        out_shape=(jax.ShapeDtypeStruct((rows, k), jnp.float32),
                   jax.ShapeDtypeStruct((k, k), jnp.float32)),
        in_specs=[pl.BlockSpec(memory_space=pl.ANY)] * 2,
        out_specs=(pl.BlockSpec(memory_space=pltpu.VMEM),) * 2,
        scratch_shapes=[
            pltpu.VMEM(snapshots.shape, snapshots.dtype),
            pltpu.VMEM(sketch.shape, sketch.dtype),
            pltpu.VMEM((nx, rows, k), jnp.float32),
            pltpu.VMEM((nx, rows, k), jnp.float32),
            pltpu.VMEM((k, k), jnp.float32),
            pltpu.VMEM((nq, c1, k), jnp.float32),
            pltpu.VMEM((c1, k), jnp.float32),
            pltpu.VMEM((nz, c1, k), jnp.float32),
            pltpu.VMEM((k, k), jnp.float32),
            dma((nx,)), dma((nx,)), dma((nx + 1,)),
            dma((nq,)), dma((nq,)), dma((nz,)), dma((nz,)), dma((nq,)), dma((nq,)),
        ],
        compiler_params=pltpu.CompilerParams(collective_id=0, has_side_effects=True),
    )(snapshots, sketch)


def factor_kernel(b, scale, g_ref, q_ref, r_ref, basis_ref, tri_ref, l_ref, w_ref):
    n = g_ref.shape[0]
    hi = lax.Precision.HIGHEST
    l_ref[...] = jnp.zeros_like(l_ref)
    w_ref[...] = jnp.zeros_like(w_ref)
    nt = (((1,), (1,)), ((), ()))
    rows = lax.broadcasted_iota(jnp.int32, (b, b), 0)
    cols = lax.broadcasted_iota(jnp.int32, (b, b), 1)

    def panel(p, carry):
        r0 = pl.multiple_of(p * b, b)
        arow = g_ref[pl.ds(r0, b), :]
        w = w_ref[...]
        x = lax.dot_general(arow, w, nt, precision=hi, preferred_element_type=jnp.float32)
        pick = (lax.broadcasted_iota(jnp.int32, (n, b), 0)
                == r0 + lax.broadcasted_iota(jnp.int32, (n, b), 1)).astype(jnp.float32)
        place = (lax.broadcasted_iota(jnp.int32, (b, n), 1)
                 == r0 + lax.broadcasted_iota(jnp.int32, (b, n), 0)).astype(jnp.float32)
        s = jnp.dot(arow, pick, precision=hi, preferred_element_type=jnp.float32)
        s = s - lax.dot_general(x, x, nt, precision=hi, preferred_element_type=jnp.float32)
        low = jnp.zeros((b, b), jnp.float32)
        inv = jnp.zeros((b, b), jnp.float32)
        rest = (rows == cols).astype(jnp.float32)
        for i in range(b):
            pivot = s[i:i + 1, i:i + 1]
            left = s[:, i:i + 1]
            s = s - left * (s[i:i + 1, :] * (1.0 / pivot))
            col = jnp.where(rows[:, i:i + 1] >= i, left / jnp.sqrt(pivot), 0.0)
            low = jnp.where(cols == i, col, low)
            irow = rest[i:i + 1, :] / col[i:i + 1, :]
            inv = jnp.where(rows == i, irow, inv)
            rest = rest - col * irow
        l_ref[pl.ds(r0, b), :] = x + jnp.dot(low, place, precision=hi,
                                             preferred_element_type=jnp.float32)
        y = jnp.dot(x, w, precision=hi, preferred_element_type=jnp.float32)
        w_ref[pl.ds(r0, b), :] = jnp.dot(inv, place - y, precision=hi,
                                         preferred_element_type=jnp.float32)
        return carry

    lax.fori_loop(0, n // b, panel, 0)
    rotated = lax.dot_general(w_ref[...], r_ref[...], (((0,), (0,)), ((), ())), precision=hi,
                              preferred_element_type=jnp.float32)
    basis_ref[...] = scale * jnp.dot(q_ref[...], rotated, precision=hi,
                                     preferred_element_type=jnp.float32)
    tri_ref[...] = l_ref[...].T / scale


def factor(gram, sketched, rotation, scale, b=128):
    n = gram.shape[0]
    return pl.pallas_call(
        functools.partial(factor_kernel, b, scale),
        out_shape=(jax.ShapeDtypeStruct(sketched.shape, jnp.float32),
                   jax.ShapeDtypeStruct((n, n), jnp.float32)),
        in_specs=[pl.BlockSpec(memory_space=pltpu.VMEM)] * 3,
        out_specs=(pl.BlockSpec(memory_space=pltpu.VMEM),) * 2,
        scratch_shapes=[pltpu.VMEM((n, n), jnp.float32)] * 2,
    )(gram, sketched, rotation)


def shards(sizes, snapshots, sketch, rotation):
    sketched, gram = sketch_and_gram(snapshots, sketch, sizes)
    cell_count = sketched.shape[0] * sizes[0] * sizes[1] * sizes[2] * sizes[3]
    scale = float(np.sqrt(np.float32(cell_count)))
    basis, triangle = factor(gram, sketched, rotation, scale)
    return (basis, triangle)


def physical_mesh(mesh):
    space, tm = mesh.devices.shape
    nc = 2
    ny = 4 if space % 8 == 0 else 1
    nz = space // (ny * nc)
    devs = mesh.devices.reshape(nz, ny, nc, tm)
    return Mesh(devs, AXES), (nz, ny, nc, tm)


def solution(mesh):
    m4, sizes = physical_mesh(mesh)
    in_specs = (P(SPACE, "x"), P("x", None), P())
    out_specs = (P(AXES, None), P())
    return jax.shard_map(functools.partial(shards, sizes), mesh=m4, in_specs=in_specs,
                         out_specs=out_specs, check_vma=False)
```

time: 101 us -> 95.3 us (0.944)
  local copies, waits for them, and re-layouts: 2.54 us -> 0 us
  matrix products: 1.73 us -> 0 us
  Pallas kernels: 96 us -> 94.5 us
    unnamed x6 -> x0, local copies, waits for them, and re-layouts: 2.54 us -> none
    dot_general x1 -> x0, matrix products: 1.73 us -> none  [shards(): lax.dot_general(sketched, sketched, (((0,), (0,)), ((), ())), precision=l...]
    pallas_call x2 -> x1, Pallas kernels: 68 us -> 66.6 us  [sketch_and_gram(): pl.pallas_call(functools.partial(fused_kernel, sizes), out_shape=(jax.Sha...]
where the time goes in v13:
time: 95.3 us; the launch traced here: 95.1 us
  Pallas kernels  94.5 us (99%)
    pallas_call x1, Pallas kernels, sketch_and_gram(): pl.pallas_call(functools.partial(fused_kernel, sizes), out_shape=(jax.Sha...  66.6 us
    pallas_call x1, Pallas kernels, factor(): pl.pallas_call(functools.partial(factor_kernel, b, scale), out_shape=(jax...  27.9 us

profile of v13, /device:TPU:1, one launch (start us, length us, event | category | flops | bytes accessed | tf_op | source)
XLA Modules:
  0.0 95.1 jit_solution(6560504541756719395)
XLA Ops:
  0.6 66.6 %shard_map.50 = (f32[512,256]{1,0:T(8,128)}, f32[256,256]{1,0:T(8,128)}) custom-call(bf16[2048,512]{1,0:T(8,128)(2,1)} %s_hbm.1, bf16[512,256]{1,0:T(8,128)(2,1)} %k_hbm.1), custom_call_target="tpu_custom_call" | custom-call | tf_op jit(solution)/shard_map/pallas_call | solution.py:126
  67.2 27.9 %shard_map.51 = (f32[512,256]{1,0:T(8,128)}, f32[256,256]{1,0:T(8,128)}) custom-call(f32[256,256]{1,0:T(8,128)} %get-tuple-element.4.g_ref, f32[512,256]{1,0:T(8,128)} %get-tuple-element.5.q_ref, f32[256,256]{1,0:T(8,128)} %r_ref.1), custom_call_target="tpu_custom_call" | custom-call | tf_op jit(solution)/shard_map/pallas_call | solution.py:198

commit v14 on v13

--- a/solution.py
+++ b/solution.py
@@ -106,14 +106,45 @@
     exchange(nq, qi, qdev, lambda j: a_ref.at[pl.ds(j * c1, c1)], lambda j: qbuf.at[j], qr, qs)
     qsum[...] = ordered_sum(qbuf, nq)
 
+    h = a_ref.shape[1] // 2
+    width = ((0, 2 * h), (h, h))
     zbuf[zi] = qsum[...]
-    exchange(nz, zi, zdev, lambda j: qsum, lambda j: zbuf.at[j], zr, zs)
+    for c, (lo, n) in enumerate(width):
+        pl.when(ci == c)(lambda lo=lo, n=n: exchange(
+            nz, zi, zdev, lambda j: qsum.at[:, pl.ds(lo, n)],
+            lambda j: zbuf.at[j, :, pl.ds(lo, n)], zr, zs))
     own = qi * c1
     full[pl.ds(own, c1)] = ordered_sum(zbuf, nz)
 
-    exchange(nq, qi, qdev, lambda j: full.at[pl.ds(own, c1)],
-             lambda j: full.at[pl.ds(j * c1, c1)], qgr, qgs)
+    per = nq // nc
+
+    def gather_copy(j, lo, n):
+        return pltpu.make_async_remote_copy(
+            src_ref=full.at[pl.ds(own, c1), pl.ds(lo, n)],
+            dst_ref=full.at[pl.ds(own, c1), pl.ds(lo, n)], send_sem=qgs.at[j],
+            recv_sem=qgr.at[qi], device_id=qdev(j), device_id_type=MESH)
+
+    for c, (lo, n) in enumerate(width):
+        def start(lo=lo, n=n):
+            for j in peers(nq, qi):
+                gather_copy(j, lo, n).start()
+        pl.when(ci == c)(start)
+    for c, (lo, n) in enumerate(width):
+        for r in range(per):
+            j = c * per + r
+            def arrived(j=j, lo=lo, n=n):
+                pltpu.make_async_remote_copy(
+                    src_ref=full.at[pl.ds(j * c1, c1), pl.ds(lo, n)],
+                    dst_ref=full.at[pl.ds(j * c1, c1), pl.ds(lo, n)], send_sem=qgs.at[j],
+                    recv_sem=qgr.at[j], device_id=qdev(j), device_id_type=MESH).wait_recv()
+            pl.when(qi != j)(arrived)
+    for c, (lo, n) in enumerate(width):
+        def sent(lo=lo, n=n):
+            for j in peers(nq, qi):
+                gather_copy(j, lo, n).wait_send()
+        pl.when(ci == c)(sent)
     g_out[...] = full[...]
+    g_out[h:, 0:h] = full[0:h, h:].T
 
 
 def sketch_and_gram(snapshots, sketch, sizes):

time: 95.3 us -> 95.9 us (level)
  no operation moved by 1% of the time
where the time goes in v14:
time: 95.9 us; the launch traced here: 95.8 us
  Pallas kernels  95.1 us (99%)
    pallas_call x1, Pallas kernels, sketch_and_gram(): pl.pallas_call(functools.partial(fused_kernel, sizes), out_shape=(jax.Sha...  67.2 us
    pallas_call x1, Pallas kernels, factor(): pl.pallas_call(functools.partial(factor_kernel, b, scale), out_shape=(jax...  27.9 us

profile of v14, /device:TPU:1, one launch (start us, length us, event | category | flops | bytes accessed | tf_op | source)
XLA Modules:
  0.0 95.8 jit_solution(7505709592909360863)
XLA Ops:
  0.6 67.2 %shard_map.50 = (f32[512,256]{1,0:T(8,128)}, f32[256,256]{1,0:T(8,128)}) custom-call(bf16[2048,512]{1,0:T(8,128)(2,1)} %s_hbm.1, bf16[512,256]{1,0:T(8,128)(2,1)} %k_hbm.1), custom_call_target="tpu_custom_call" | custom-call | tf_op jit(solution)/shard_map/pallas_call | solution.py:157
  67.9 27.9 %shard_map.51 = (f32[512,256]{1,0:T(8,128)}, f32[256,256]{1,0:T(8,128)}) custom-call(f32[256,256]{1,0:T(8,128)} %get-tuple-element.4.g_ref, f32[512,256]{1,0:T(8,128)} %get-tuple-element.5.q_ref, f32[256,256]{1,0:T(8,128)} %r_ref.1), custom_call_target="tpu_custom_call" | custom-call | tf_op jit(solution)/shard_map/pallas_call | solution.py:229

commit v15 on v13

--- a/solution.py
+++ b/solution.py
@@ -47,22 +47,25 @@
         pltpu.make_async_copy(s_hbm.at[pl.ds(j * rows, rows)],
                               s_ref.at[pl.ds(j * rows, rows)], ls.at[j]).wait()
 
-    pl.semaphore_wait(barrier, count)
-
-    copies = []
     for d in range(1, nx):
         j = lax.rem(xi + d, nx)
         fetched(j)
         block = s_ref[pl.ds(pl.multiple_of(j * rows, rows), rows), :]
         part[j] = jnp.dot(block, k_ref[...], preferred_element_type=jnp.float32)
+    fetched(xi)
+    block = s_ref[pl.ds(pl.multiple_of(xi * rows, rows), rows), :]
+    rbuf[xi] = jnp.dot(block, k_ref[...], preferred_element_type=jnp.float32)
+
+    pl.semaphore_wait(barrier, count)
+
+    copies = []
+    for d in range(1, nx):
+        j = lax.rem(xi + d, nx)
         cp = pltpu.make_async_remote_copy(
             src_ref=part.at[j], dst_ref=rbuf.at[xi], send_sem=ss.at[j],
             recv_sem=rs.at[xi], device_id=xdev(j), device_id_type=MESH)
         cp.start()
         copies.append(cp)
-    fetched(xi)
-    block = s_ref[pl.ds(pl.multiple_of(xi * rows, rows), rows), :]
-    rbuf[xi] = jnp.dot(block, k_ref[...], preferred_element_type=jnp.float32)
     for d in range(1, nx):
         j = lax.rem(xi + d, nx)
         pltpu.make_async_remote_copy(

time: 95.3 us -> 94.9 us (level)
  no operation moved by 1% of the time
where the time goes in v15:
time: 94.9 us; the launch traced here: 94.7 us
  Pallas kernels  94.1 us (99%)
    pallas_call x1, Pallas kernels, sketch_and_gram(): pl.pallas_call(functools.partial(fused_kernel, sizes), out_shape=(jax.Sha...  66.2 us
    pallas_call x1, Pallas kernels, factor(): pl.pallas_call(functools.partial(factor_kernel, b, scale), out_shape=(jax...  27.9 us

profile of v15, /device:TPU:1, one launch (start us, length us, event | category | flops | bytes accessed | tf_op | source)
XLA Modules:
  0.0 94.7 jit_solution(17437144408561011453)
XLA Ops:
  0.6 66.2 %shard_map.50 = (f32[512,256]{1,0:T(8,128)}, f32[256,256]{1,0:T(8,128)}) custom-call(bf16[2048,512]{1,0:T(8,128)(2,1)} %s_hbm.1, bf16[512,256]{1,0:T(8,128)(2,1)} %k_hbm.1), custom_call_target="tpu_custom_call" | custom-call | tf_op jit(solution)/shard_map/pallas_call | solution.py:129
  66.8 27.9 %shard_map.51 = (f32[512,256]{1,0:T(8,128)}, f32[256,256]{1,0:T(8,128)}) custom-call(f32[256,256]{1,0:T(8,128)} %get-tuple-element.4.g_ref, f32[512,256]{1,0:T(8,128)} %get-tuple-element.5.q_ref, f32[256,256]{1,0:T(8,128)} %r_ref.1), custom_call_target="tpu_custom_call" | custom-call | tf_op jit(solution)/shard_map/pallas_call | solution.py:201

commit v16 on v13

--- a/solution.py
+++ b/solution.py
@@ -160,11 +160,7 @@
         arow = g_ref[pl.ds(r0, b), :]
         w = w_ref[...]
         x = lax.dot_general(arow, w, nt, precision=hi, preferred_element_type=jnp.float32)
-        pick = (lax.broadcasted_iota(jnp.int32, (n, b), 0)
-                == r0 + lax.broadcasted_iota(jnp.int32, (n, b), 1)).astype(jnp.float32)
-        place = (lax.broadcasted_iota(jnp.int32, (b, n), 1)
-                 == r0 + lax.broadcasted_iota(jnp.int32, (b, n), 0)).astype(jnp.float32)
-        s = jnp.dot(arow, pick, precision=hi, preferred_element_type=jnp.float32)
+        s = g_ref[pl.ds(r0, b), pl.ds(r0, b)]
         s = s - lax.dot_general(x, x, nt, precision=hi, preferred_element_type=jnp.float32)
         low = jnp.zeros((b, b), jnp.float32)
         inv = jnp.zeros((b, b), jnp.float32)
@@ -178,11 +174,11 @@
             irow = rest[i:i + 1, :] / col[i:i + 1, :]
             inv = jnp.where(rows == i, irow, inv)
             rest = rest - col * irow
-        l_ref[pl.ds(r0, b), :] = x + jnp.dot(low, place, precision=hi,
-                                             preferred_element_type=jnp.float32)
+        l_ref[pl.ds(r0, b), :] = x
+        l_ref[pl.ds(r0, b), pl.ds(r0, b)] = low
         y = jnp.dot(x, w, precision=hi, preferred_element_type=jnp.float32)
-        w_ref[pl.ds(r0, b), :] = jnp.dot(inv, place - y, precision=hi,
-                                         preferred_element_type=jnp.float32)
+        w_ref[pl.ds(r0, b), :] = -jnp.dot(inv, y, precision=hi, preferred_element_type=jnp.float32)
+        w_ref[pl.ds(r0, b), pl.ds(r0, b)] = inv
         return carry
 
     lax.fori_loop(0, n // b, panel, 0)

time: 95.3 us -> 93.9 us (0.985)
  Pallas kernels: 94.5 us -> 93.1 us
    pallas_call x1, Pallas kernels: 27.9 us -> 26.5 us  [factor(): pl.pallas_call(functools.partial(factor_kernel, b, scale), out_shape=(jax...]
where the time goes in v16:
time: 93.9 us; the launch traced here: 93.7 us
  Pallas kernels  93.1 us (99%)
    pallas_call x1, Pallas kernels, sketch_and_gram(): pl.pallas_call(functools.partial(fused_kernel, sizes), out_shape=(jax.Sha...  66.6 us
    pallas_call x1, Pallas kernels, factor(): pl.pallas_call(functools.partial(factor_kernel, b, scale), out_shape=(jax...  26.5 us

profile of v16, /device:TPU:1, one launch (start us, length us, event | category | flops | bytes accessed | tf_op | source)
XLA Modules:
  0.0 93.7 jit_solution(15050568363209239238)
XLA Ops:
  0.6 66.6 %shard_map.50 = (f32[512,256]{1,0:T(8,128)}, f32[256,256]{1,0:T(8,128)}) custom-call(bf16[2048,512]{1,0:T(8,128)(2,1)} %s_hbm.1, bf16[512,256]{1,0:T(8,128)(2,1)} %k_hbm.1), custom_call_target="tpu_custom_call" | custom-call | tf_op jit(solution)/shard_map/pallas_call | solution.py:126
  67.2 26.5 %shard_map.51 = (f32[512,256]{1,0:T(8,128)}, f32[256,256]{1,0:T(8,128)}) custom-call(f32[256,256]{1,0:T(8,128)} %get-tuple-element.4.g_ref, f32[512,256]{1,0:T(8,128)} %get-tuple-element.5.q_ref, f32[256,256]{1,0:T(8,128)} %r_ref.1), custom_call_target="tpu_custom_call" | custom-call | tf_op jit(solution)/shard_map/pallas_call | solution.py:194

commit v17 on v16

--- a/solution.py
+++ b/solution.py
@@ -146,7 +146,7 @@
     )(snapshots, sketch)
 
 
-def factor_kernel(b, scale, g_ref, q_ref, r_ref, basis_ref, tri_ref, l_ref, w_ref):
+def factor_kernel(b, scale, g_ref, q_ref, r_ref, basis_ref, tri_ref, l_ref, w_ref, s_ref):
     n = g_ref.shape[0]
     hi = lax.Precision.HIGHEST
     l_ref[...] = jnp.zeros_like(l_ref)
@@ -157,11 +157,17 @@
 
     def panel(p, carry):
         r0 = pl.multiple_of(p * b, b)
-        arow = g_ref[pl.ds(r0, b), :]
-        w = w_ref[...]
-        x = lax.dot_general(arow, w, nt, precision=hi, preferred_element_type=jnp.float32)
-        s = g_ref[pl.ds(r0, b), pl.ds(r0, b)]
-        s = s - lax.dot_general(x, x, nt, precision=hi, preferred_element_type=jnp.float32)
+        s_ref[...] = g_ref[pl.ds(r0, b), pl.ds(r0, b)]
+
+        @pl.when(p > 0)
+        def _():
+            x = lax.dot_general(g_ref[pl.ds(r0, b), :], w_ref[...], nt, precision=hi,
+                                preferred_element_type=jnp.float32)
+            l_ref[pl.ds(r0, b), :] = x
+            s_ref[...] -= lax.dot_general(x, x, nt, precision=hi,
+                                          preferred_element_type=jnp.float32)
+
+        s = s_ref[...]
         low = jnp.zeros((b, b), jnp.float32)
         inv = jnp.zeros((b, b), jnp.float32)
         rest = (rows == cols).astype(jnp.float32)
@@ -174,10 +180,15 @@
             irow = rest[i:i + 1, :] / col[i:i + 1, :]
             inv = jnp.where(rows == i, irow, inv)
             rest = rest - col * irow
-        l_ref[pl.ds(r0, b), :] = x
+
+        @pl.when(p > 0)
+        def _():
+            y = jnp.dot(l_ref[pl.ds(r0, b), :], w_ref[...], precision=hi,
+                        preferred_element_type=jnp.float32)
+            w_ref[pl.ds(r0, b), :] = -jnp.dot(inv, y, precision=hi,
+                                              preferred_element_type=jnp.float32)
+
         l_ref[pl.ds(r0, b), pl.ds(r0, b)] = low
-        y = jnp.dot(x, w, precision=hi, preferred_element_type=jnp.float32)
-        w_ref[pl.ds(r0, b), :] = -jnp.dot(inv, y, precision=hi, preferred_element_type=jnp.float32)
         w_ref[pl.ds(r0, b), pl.ds(r0, b)] = inv
         return carry
 
@@ -197,7 +208,7 @@
                    jax.ShapeDtypeStruct((n, n), jnp.float32)),
         in_specs=[pl.BlockSpec(memory_space=pltpu.VMEM)] * 3,
         out_specs=(pl.BlockSpec(memory_space=pltpu.VMEM),) * 2,
-        scratch_shapes=[pltpu.VMEM((n, n), jnp.float32)] * 2,
+        scratch_shapes=[pltpu.VMEM((n, n), jnp.float32)] * 2 + [pltpu.VMEM((b, b), jnp.float32)],
     )(gram, sketched, rotation)
 
 

time: 93.9 us -> 92.9 us (0.989)
  Pallas kernels: 93.1 us -> 92.1 us
    pallas_call x1, Pallas kernels: 26.5 us -> 25.5 us  [factor(): pl.pallas_call(functools.partial(factor_kernel, b, scale), out_shape=(jax...]
where the time goes in v17:
time: 92.9 us; the launch traced here: 92.7 us
  Pallas kernels  92.1 us (99%)
    pallas_call x1, Pallas kernels, sketch_and_gram(): pl.pallas_call(functools.partial(fused_kernel, sizes), out_shape=(jax.Sha...  66.6 us
    pallas_call x1, Pallas kernels, factor(): pl.pallas_call(functools.partial(factor_kernel, b, scale), out_shape=(jax...  25.5 us

profile of v17, /device:TPU:1, one launch (start us, length us, event | category | flops | bytes accessed | tf_op | source)
XLA Modules:
  0.0 92.7 jit_solution(13545780992202411473)
XLA Ops:
  0.6 66.6 %shard_map.50 = (f32[512,256]{1,0:T(8,128)}, f32[256,256]{1,0:T(8,128)}) custom-call(bf16[2048,512]{1,0:T(8,128)(2,1)} %s_hbm.1, bf16[512,256]{1,0:T(8,128)(2,1)} %k_hbm.1), custom_call_target="tpu_custom_call" | custom-call | tf_op jit(solution)/shard_map/pallas_call | solution.py:126
  67.2 25.5 %shard_map.51 = (f32[512,256]{1,0:T(8,128)}, f32[256,256]{1,0:T(8,128)}) custom-call(f32[256,256]{1,0:T(8,128)} %get-tuple-element.4.g_ref, f32[512,256]{1,0:T(8,128)} %get-tuple-element.5.q_ref, f32[256,256]{1,0:T(8,128)} %r_ref.1), custom_call_target="tpu_custom_call" | custom-call | tf_op jit(solution)/shard_map/pallas_call | solution.py:205

commit v18 on v17

--- a/solution.py
+++ b/solution.py
@@ -193,9 +193,9 @@
         return carry
 
     lax.fori_loop(0, n // b, panel, 0)
-    rotated = lax.dot_general(w_ref[...], r_ref[...], (((0,), (0,)), ((), ())), precision=hi,
-                              preferred_element_type=jnp.float32)
-    basis_ref[...] = scale * jnp.dot(q_ref[...], rotated, precision=hi,
+    orthonormal = lax.dot_general(q_ref[...], w_ref[...], nt, precision=hi,
+                                  preferred_element_type=jnp.float32)
+    basis_ref[...] = scale * jnp.dot(orthonormal, r_ref[...], precision=hi,
                                      preferred_element_type=jnp.float32)
     tri_ref[...] = l_ref[...].T / scale
 

time: 92.9 us -> 93.4 us (level)
  no operation moved by 1% of the time
where the time goes in v18:
time: 93.4 us; the launch traced here: 93.2 us
  Pallas kernels  92.6 us (99%)
    pallas_call x1, Pallas kernels, sketch_and_gram(): pl.pallas_call(functools.partial(fused_kernel, sizes), out_shape=(jax.Sha...  66.6 us
    pallas_call x1, Pallas kernels, factor(): pl.pallas_call(functools.partial(factor_kernel, b, scale), out_shape=(jax...  26 us

profile of v18, /device:TPU:1, one launch (start us, length us, event | category | flops | bytes accessed | tf_op | source)
XLA Modules:
  0.0 93.2 jit_solution(9851585918597248313)
XLA Ops:
  0.6 66.6 %shard_map.50 = (f32[512,256]{1,0:T(8,128)}, f32[256,256]{1,0:T(8,128)}) custom-call(bf16[2048,512]{1,0:T(8,128)(2,1)} %s_hbm.1, bf16[512,256]{1,0:T(8,128)(2,1)} %k_hbm.1), custom_call_target="tpu_custom_call" | custom-call | tf_op jit(solution)/shard_map/pallas_call | solution.py:126
  67.2 26.0 %shard_map.51 = (f32[512,256]{1,0:T(8,128)}, f32[256,256]{1,0:T(8,128)}) custom-call(f32[256,256]{1,0:T(8,128)} %get-tuple-element.4.g_ref, f32[512,256]{1,0:T(8,128)} %get-tuple-element.5.q_ref, f32[256,256]{1,0:T(8,128)} %r_ref.1), custom_call_target="tpu_custom_call" | custom-call | tf_op jit(solution)/shard_map/pallas_call | solution.py:205
